TPU v7x, 32 devices: a whole 2x2x4 slice. The times are simulated.
32 devices in a mesh: tm: 2 (over core), space: 16 (over z, y, x).
Axes of the slice: x: 2, y: 2, z: 4, core: 2. Of those that a mesh axis runs over, the one named last changes fastest.
Arguments:
- slab_starts: float32 [2, 64, 24, 512], P('tm', 'space'), may hold values from -6 to 6
- forcing: float32 [2, 2, 64, 24, 512], P('tm', None, 'space'), may hold values from -5 to 5
- density: float32 [64, 24, 512], P('space'), may hold values from 0.25 to 4
- moving_flags: int32 [64, 24, 512], P('space'), may hold values 0 or 1
Outputs:
- new_starts: float32 [2, 64, 24, 512], P('tm', 'space')
- new_interior: float32 [2, 64, 24, 512], P('tm', 'space')
All inputs are finite; a program needn't handle non-finite values. No bound on the sum of `moving_flags` on one device may be relied on, other than what follows from the above.
Results may differ from a plain program's by a relative error of at most 0.0001.
Values sent between devices are 32-bit elements; how exact they have to be, the bound alone decides.
A program may use at most 64 MiB of HBM per device.

v0:
```python
import jax
import jax.numpy as jnp
from jax import lax
from jax.sharding import PartitionSpec as P

COARSE_SWEEPS = 4


STIFFNESS = 4.0
COARSE_STIFF = 0.25
FORCE_WEIGHT = 0.5
RELAX = 0.8
MASS_FLAG = 3.0


def padded(block, sides, width):
    for axis, dim in sides:
        count = lax.axis_size(axis)
        forward = [(i, i + 1) for i in range(count - 1)]
        backward = [(target, source) for source, target in forward]
        low = lax.ppermute(
            lax.slice_in_dim(block, block.shape[dim] - width, None, axis=dim), axis, forward
        )
        high = lax.ppermute(lax.slice_in_dim(block, 0, width, axis=dim), axis, backward)
        block = jnp.concatenate([low, block, high], axis=dim)
    return block


def from_behind(value, axis, steps):
    count = lax.axis_size(axis)
    pairs = [(source, (source + steps) % count) for source in range(count)]
    return lax.ppermute(value, axis, pairs)


def shrink(field):
    a, b, c = field.shape
    return field.reshape(a // 2, 2, b // 2, 2, c // 2, 2).mean(axis=(1, 3, 5))


def expand(field):
    return jnp.repeat(jnp.repeat(jnp.repeat(field, 2, axis=0), 2, axis=1), 2, axis=2)


def plane_sum(extended):
    inner = extended[1:-1]
    side = jnp.pad(inner, ((0, 0), (1, 1), (1, 1)))
    total = extended[2:] + extended[:-2]
    total = total + side[:, 2:, 1:-1] + side[:, :-2, 1:-1]
    return total + side[:, 1:-1, 2:] + side[:, 1:-1, :-2]


def fine_operate(field, mass, conduct):
    extended = padded(field, (("space", 0),), 1)
    return mass * field + STIFFNESS * conduct * (6.0 * field - plane_sum(extended))


def coarse_operate(field, mass_c, conduct_c):
    extended = padded(field, (("space", 0),), 1)
    return mass_c * field + COARSE_STIFF * conduct_c * (6.0 * field - plane_sum(extended))


def coarse_solve(coarse_rhs, coeffs):
    mass_c, conduct_c, block_mass, block_conduct = coeffs
    diag_c = mass_c + 6.0 * COARSE_STIFF * conduct_c
    error = RELAX * coarse_rhs / diag_c
    for sweep in range(COARSE_SWEEPS - 1):
        error = error + RELAX * (coarse_rhs - coarse_operate(error, mass_c, conduct_c)) / diag_c
    return error


def advance(prior, source, mass, conduct, diag, coeffs):
    rhs = mass * prior + FORCE_WEIGHT * source
    state = prior
    state = state + RELAX * (rhs - fine_operate(state, mass, conduct)) / diag
    resid = rhs - fine_operate(state, mass, conduct)
    coarse_rhs = shrink(shrink(resid))
    error = coarse_solve(coarse_rhs, coeffs)
    state = state + expand(expand(error))
    return state


def local(slab_starts, forcing, density, moving_flags):
    conduct = 1.0 / density
    mass = 1.0 + MASS_FLAG * moving_flags.astype(jnp.float32)
    diag = mass + 6.0 * STIFFNESS * conduct
    mass_c = shrink(shrink(mass))
    conduct_c = shrink(shrink(conduct))
    block_mass, block_conduct = (mass_c, conduct_c)
    coeffs = (mass_c, conduct_c, block_mass, block_conduct)
    middle = advance(slab_starts[0], forcing[0, 0], mass, conduct, diag, coeffs)
    ending = advance(middle, forcing[0, 1], mass, conduct, diag, coeffs)
    arrived = from_behind(ending, "tm", 1)
    interior = advance(arrived, forcing[0, 0], mass, conduct, diag, coeffs)
    return (arrived[None], interior[None])


def solution(mesh):
    placed = (
        P("tm", "space", None, None),
        P("tm", None, "space", None, None),
        P("space", None, None),
        P("space", None, None),
    )
    return jax.shard_map(
        local,
        mesh=mesh,
        in_specs=placed,
        out_specs=(P("tm", "space", None, None), P("tm", "space", None, None)),
        check_vma=False,
    )
```

profile of v0, /device:TPU:24, one launch (start us, length us, event | category | flops | bytes accessed | tf_op | source)
XLA Modules:
  0.0 254.2 jit_solution(810459349092430169)
XLA Ops:
  1.5 4.2 %collective-permute-start = (f32[1,24,512]{2,1,0:T(8,128)S(1)}, f32[1,24,512]{2,1,0:T(8,128)S(1)}, u32[]{:S(2)}, u32[]{:S(2)}) collective-permute-start(f32[1,24,512]{2,1,0:T(8,128)S(1)} %get-tuple-element.15), channel_id=1, source_target_pairs={{1,0},{2,1},{3,2},{4,3},{5,4},{6,5},{7,6},{8,7},{9,8},{10,9},{11,1... | collective-permute-start | bytes 147464 | tf_op jit(solution)/shard_map/ppermute | solution.py:24
  5.7 1.9 collective-permute-start.1
  7.6 5.8 %collective-permute-done.1 = f32[1,24,512]{2,1,0:T(8,128)S(1)} collective-permute-done((f32[1,24,512]{2,1,0:T(8,128)S(1)}, f32[1,24,512]{2,1,0:T(8,128)S(1)}, u32[]{:S(2)}, u32[]{:S(2)}) %collective-permute-start.1) | collective-permute-done | bytes 49184 | tf_op jit(solution)/shard_map/ppermute | solution.py:21
  13.5 1.9 multiply_add_fusion.1
  15.4 1.9 collective-permute-start.2
  17.4 3.9 %collective-permute-start.3 = (f32[1,24,512]{2,1,0:T(8,128)S(1)}, f32[1,24,512]{2,1,0:T(8,128)S(1)}, u32[]{:S(2)}, u32[]{:S(2)}) collective-permute-start(f32[1,24,512]{2,1,0:T(8,128)S(1)} %get-tuple-element.14), channel_id=1, source_target_pairs={{0,1},{1,2},{2,3},{3,4},{4,5},{5,6},{6,7},{7,8},{8,9},{9,10},{10,1... | collective-permute-start | bytes 147464 | tf_op jit(solution)/shard_map/ppermute | solution.py:21
  21.3 13.9 %reshape.284 = f32[2,2,12,2,256,2]{5,4,3,2,1,0:T(8,128)} reshape(f32[4,24,512]{2,1,0:T(8,128)S(1)} %get-tuple-element.10) | data formatting | bytes 393216 | tf_op jit(solution)/shard_map/reshape | solution.py:37
  35.2 5.5 %reduce_sum.109 = f32[2,12,256]{2,1,0:T(8,128)S(1)} reduce(f32[2,2,12,2,256,2]{5,4,3,2,1,0:T(8,128)} %reshape.284, f32[]{:T(128)} %constant.36.clone.1), dimensions={1,3,5}, to_apply=%region_3.0 | reduce | flops 43008 | bytes 221188 | tf_op jit(solution)/shard_map/reduce_sum | solution.py:37
  40.7 13.9 %reshape.285 = f32[2,2,12,2,256,2]{5,4,3,2,1,0:T(8,128)} reshape(f32[4,24,512]{2,1,0:T(8,128)S(1)} %get-tuple-element.12) | data formatting | bytes 393216 | tf_op jit(solution)/shard_map/reshape | solution.py:37
  54.6 5.5 %reduce_sum.133 = f32[2,12,256]{2,1,0:T(8,128)S(1)} reduce(f32[2,2,12,2,256,2]{5,4,3,2,1,0:T(8,128)} %reshape.285, f32[]{:T(128)} %constant.36.clone.1), dimensions={1,3,5}, to_apply=%region_6.7 | reduce | flops 43008 | bytes 221188 | tf_op jit(solution)/shard_map/reduce_sum | solution.py:37
  62.3 13.9 %reshape.283 = f32[2,2,12,2,256,2]{5,4,3,2,1,0:T(8,128)} reshape(f32[4,24,512]{2,1,0:T(8,128)S(1)} %fusion.18) | data formatting | bytes 393216 | tf_op jit(solution)/shard_map/reshape | solution.py:37
  76.2 5.5 %reduce_sum.102 = f32[2,12,256]{2,1,0:T(8,128)S(1)} reduce(f32[2,2,12,2,256,2]{5,4,3,2,1,0:T(8,128)} %reshape.283, f32[]{:T(128)} %constant.36.clone.1), dimensions={1,3,5}, to_apply=%region_0.0 | reduce | flops 43008 | bytes 221188 | tf_op jit(solution)/shard_map/reduce_sum | solution.py:37
  82.6 3.7 %collective-permute-start.4 = (f32[1,6,128]{2,1,0:T(8,128)S(1)}, f32[1,6,128]{2,1,0:T(8,128)S(1)}, u32[]{:S(2)}, u32[]{:S(2)}) collective-permute-start(f32[1,6,128]{2,1,0:T(8,128)S(1)} %bitcast_divide_fusion.2), channel_id=1, source_target_pairs={{1,0},{2,1},{3,2},{4,3},{5,4},{6,5},{7,6},{8,7},{9,8},{10,9},{11,1... | collective-permute-start | bytes 9224 | tf_op jit(solution)/shard_map/ppermute | solution.py:24
  86.4 2.1 collective-permute-start.5
  88.5 5.2 %collective-permute-done.5 = f32[1,6,128]{2,1,0:T(8,128)S(1)} collective-permute-done((f32[1,6,128]{2,1,0:T(8,128)S(1)}, f32[1,6,128]{2,1,0:T(8,128)S(1)}, u32[]{:S(2)}, u32[]{:S(2)}) %collective-permute-start.5) | collective-permute-done | bytes 3104 | tf_op jit(solution)/shard_map/ppermute | solution.py:21
  95.7 3.9 %collective-permute-start.7 = (f32[1,6,128]{2,1,0:T(8,128)S(1)}, f32[1,6,128]{2,1,0:T(8,128)S(1)}, u32[]{:S(2)}, u32[]{:S(2)}) collective-permute-start(f32[1,6,128]{2,1,0:T(8,128)S(1)} %fusion.73), channel_id=1, source_target_pairs={{0,1},{1,2},{2,3},{3,4},{4,5},{5,6},{6,7},{7,8},{8,9},{9,10},{10,1... | collective-permute-start | bytes 9224 | tf_op jit(solution)/shard_map/ppermute | solution.py:21
  99.6 3.4 %collective-permute-done.7 = f32[1,6,128]{2,1,0:T(8,128)S(1)} collective-permute-done((f32[1,6,128]{2,1,0:T(8,128)S(1)}, f32[1,6,128]{2,1,0:T(8,128)S(1)}, u32[]{:S(2)}, u32[]{:S(2)}) %collective-permute-start.7) | collective-permute-done | bytes 3104 | tf_op jit(solution)/shard_map/ppermute | solution.py:21
  105.0 3.9 %collective-permute-start.9 = (f32[1,6,128]{2,1,0:T(8,128)S(1)}, f32[1,6,128]{2,1,0:T(8,128)S(1)}, u32[]{:S(2)}, u32[]{:S(2)}) collective-permute-start(f32[1,6,128]{2,1,0:T(8,128)S(1)} %fusion.84), channel_id=1, source_target_pairs={{0,1},{1,2},{2,3},{3,4},{4,5},{5,6},{6,7},{7,8},{8,9},{9,10},{10,1... | collective-permute-start | bytes 9224 | tf_op jit(solution)/shard_map/ppermute | solution.py:21
  108.9 3.4 %collective-permute-done.9 = f32[1,6,128]{2,1,0:T(8,128)S(1)} collective-permute-done((f32[1,6,128]{2,1,0:T(8,128)S(1)}, f32[1,6,128]{2,1,0:T(8,128)S(1)}, u32[]{:S(2)}, u32[]{:S(2)}) %collective-permute-start.9) | collective-permute-done | bytes 3104 | tf_op jit(solution)/shard_map/ppermute | solution.py:21
  113.1 1.9 collective-permute-start.10
  115.0 3.9 %collective-permute-start.11 = (f32[1,24,512]{2,1,0:T(8,128)S(1)}, f32[1,24,512]{2,1,0:T(8,128)S(1)}, u32[]{:S(2)}, u32[]{:S(2)}) collective-permute-start(f32[1,24,512]{2,1,0:T(8,128)S(1)} %get-tuple-element.9), channel_id=1, source_target_pairs={{0,1},{1,2},{2,3},{3,4},{4,5},{5,6},{6,7},{7,8},{8,9},{9,10},{10,1... | collective-permute-start | bytes 147464 | tf_op jit(solution)/shard_map/ppermute | solution.py:21
  119.1 3.7 %collective-permute-done.11 = f32[1,24,512]{2,1,0:T(8,128)S(1)} collective-permute-done((f32[1,24,512]{2,1,0:T(8,128)S(1)}, f32[1,24,512]{2,1,0:T(8,128)S(1)}, u32[]{:S(2)}, u32[]{:S(2)}) %collective-permute-start.11) | collective-permute-done | bytes 49184 | tf_op jit(solution)/shard_map/ppermute | solution.py:21
  123.0 2.1 collective-permute-start.12
  125.2 3.9 %collective-permute-start.13 = (f32[1,24,512]{2,1,0:T(8,128)S(1)}, f32[1,24,512]{2,1,0:T(8,128)S(1)}, u32[]{:S(2)}, u32[]{:S(2)}) collective-permute-start(f32[1,24,512]{2,1,0:T(8,128)S(1)} %get-tuple-element.7), channel_id=1, source_target_pairs={{0,1},{1,2},{2,3},{3,4},{4,5},{5,6},{6,7},{7,8},{8,9},{9,10},{10,1... | collective-permute-start | bytes 147464 | tf_op jit(solution)/shard_map/ppermute | solution.py:21
  129.1 3.9 %collective-permute-done.13 = f32[1,24,512]{2,1,0:T(8,128)S(1)} collective-permute-done((f32[1,24,512]{2,1,0:T(8,128)S(1)}, f32[1,24,512]{2,1,0:T(8,128)S(1)}, u32[]{:S(2)}, u32[]{:S(2)}) %collective-permute-start.13) | collective-permute-done | bytes 49184 | tf_op jit(solution)/shard_map/ppermute | solution.py:21
  133.2 13.9 %reshape.286 = f32[2,2,12,2,256,2]{5,4,3,2,1,0:T(8,128)} reshape(f32[4,24,512]{2,1,0:T(8,128)S(1)} %fusion.37) | data formatting | bytes 393216 | tf_op jit(solution)/shard_map/reshape | solution.py:37
  147.1 5.5 %reduce_sum.137 = f32[2,12,256]{2,1,0:T(8,128)S(1)} reduce(f32[2,2,12,2,256,2]{5,4,3,2,1,0:T(8,128)} %reshape.286, f32[]{:T(128)} %constant.36.clone.1), dimensions={1,3,5}, to_apply=%region_9.10 | reduce | flops 43008 | bytes 221188 | tf_op jit(solution)/shard_map/reduce_sum | solution.py:37
  155.5 3.9 %collective-permute-start.15 = (f32[1,6,128]{2,1,0:T(8,128)S(1)}, f32[1,6,128]{2,1,0:T(8,128)S(1)}, u32[]{:S(2)}, u32[]{:S(2)}) collective-permute-start(f32[1,6,128]{2,1,0:T(8,128)S(1)} %bitcast_divide_fusion.1), channel_id=1, source_target_pairs={{0,1},{1,2},{2,3},{3,4},{4,5},{5,6},{6,7},{7,8},{8,9},{9,10},{10,1... | collective-permute-start | bytes 9224 | tf_op jit(solution)/shard_map/ppermute | solution.py:21
  159.4 3.4 %collective-permute-done.15 = f32[1,6,128]{2,1,0:T(8,128)S(1)} collective-permute-done((f32[1,6,128]{2,1,0:T(8,128)S(1)}, f32[1,6,128]{2,1,0:T(8,128)S(1)}, u32[]{:S(2)}, u32[]{:S(2)}) %collective-permute-start.15) | collective-permute-done | bytes 3104 | tf_op jit(solution)/shard_map/ppermute | solution.py:21
  162.8 2.0 collective-permute-start.16
  164.9 3.8 %collective-permute-start.17 = (f32[1,6,128]{2,1,0:T(8,128)S(1)}, f32[1,6,128]{2,1,0:T(8,128)S(1)}, u32[]{:S(2)}, u32[]{:S(2)}) collective-permute-start(f32[1,6,128]{2,1,0:T(8,128)S(1)} %fusion.106), channel_id=1, source_target_pairs={{0,1},{1,2},{2,3},{3,4},{4,5},{5,6},{6,7},{7,8},{8,9},{9,10},{10,1... | collective-permute-start | bytes 9224 | tf_op jit(solution)/shard_map/ppermute | solution.py:21
  168.7 3.5 %collective-permute-done.17 = f32[1,6,128]{2,1,0:T(8,128)S(1)} collective-permute-done((f32[1,6,128]{2,1,0:T(8,128)S(1)}, f32[1,6,128]{2,1,0:T(8,128)S(1)}, u32[]{:S(2)}, u32[]{:S(2)}) %collective-permute-start.17) | collective-permute-done | bytes 3104 | tf_op jit(solution)/shard_map/ppermute | solution.py:21
  174.2 3.9 %collective-permute-start.19 = (f32[1,6,128]{2,1,0:T(8,128)S(1)}, f32[1,6,128]{2,1,0:T(8,128)S(1)}, u32[]{:S(2)}, u32[]{:S(2)}) collective-permute-start(f32[1,6,128]{2,1,0:T(8,128)S(1)} %fusion.117), channel_id=1, source_target_pairs={{0,1},{1,2},{2,3},{3,4},{4,5},{5,6},{6,7},{7,8},{8,9},{9,10},{10,1... | collective-permute-start | bytes 9224 | tf_op jit(solution)/shard_map/ppermute | solution.py:21
  178.1 3.4 %collective-permute-done.19 = f32[1,6,128]{2,1,0:T(8,128)S(1)} collective-permute-done((f32[1,6,128]{2,1,0:T(8,128)S(1)}, f32[1,6,128]{2,1,0:T(8,128)S(1)}, u32[]{:S(2)}, u32[]{:S(2)}) %collective-permute-start.19) | collective-permute-done | bytes 3104 | tf_op jit(solution)/shard_map/ppermute | solution.py:21
  183.7 2.1 collective-permute-start.21
  185.8 3.8 %collective-permute-start.22 = (f32[1,24,512]{2,1,0:T(8,128)S(1)}, f32[1,24,512]{2,1,0:T(8,128)S(1)}, u32[]{:S(2)}, u32[]{:S(2)}) collective-permute-start(f32[1,24,512]{2,1,0:T(8,128)S(1)} %get-tuple-element.5), channel_id=1, source_target_pairs={{0,1},{1,2},{2,3},{3,4},{4,5},{5,6},{6,7},{7,8},{8,9},{9,10},{10,1... | collective-permute-start | bytes 147464 | tf_op jit(solution)/shard_map/ppermute | solution.py:21
  189.7 3.9 %collective-permute-done.22 = f32[1,24,512]{2,1,0:T(8,128)S(1)} collective-permute-done((f32[1,24,512]{2,1,0:T(8,128)S(1)}, f32[1,24,512]{2,1,0:T(8,128)S(1)}, u32[]{:S(2)}, u32[]{:S(2)}) %collective-permute-start.22) | collective-permute-done | bytes 49184 | tf_op jit(solution)/shard_map/ppermute | solution.py:21
  195.8 3.9 %collective-permute-start.24 = (f32[1,24,512]{2,1,0:T(8,128)S(1)}, f32[1,24,512]{2,1,0:T(8,128)S(1)}, u32[]{:S(2)}, u32[]{:S(2)}) collective-permute-start(f32[1,24,512]{2,1,0:T(8,128)S(1)} %get-tuple-element.3), channel_id=1, source_target_pairs={{0,1},{1,2},{2,3},{3,4},{4,5},{5,6},{6,7},{7,8},{8,9},{9,10},{10,1... | collective-permute-start | bytes 147464 | tf_op jit(solution)/shard_map/ppermute | solution.py:21
  200.1 3.5 %collective-permute-done.24 = f32[1,24,512]{2,1,0:T(8,128)S(1)} collective-permute-done((f32[1,24,512]{2,1,0:T(8,128)S(1)}, f32[1,24,512]{2,1,0:T(8,128)S(1)}, u32[]{:S(2)}, u32[]{:S(2)}) %collective-permute-start.24) | collective-permute-done | bytes 49184 | tf_op jit(solution)/shard_map/ppermute | solution.py:21
  203.8 13.9 %reshape.287 = f32[2,2,12,2,256,2]{5,4,3,2,1,0:T(8,128)} reshape(f32[4,24,512]{2,1,0:T(8,128)S(1)} %fusion.56) | data formatting | bytes 393216 | tf_op jit(solution)/shard_map/reshape | solution.py:37
  217.7 5.5 %reduce_sum.141 = f32[2,12,256]{2,1,0:T(8,128)S(1)} reduce(f32[2,2,12,2,256,2]{5,4,3,2,1,0:T(8,128)} %reshape.287, f32[]{:T(128)} %constant.36.clone.1), dimensions={1,3,5}, to_apply=%region_12.13 | reduce | flops 43008 | bytes 221188 | tf_op jit(solution)/shard_map/reduce_sum | solution.py:37
  224.1 2.1 collective-permute-start.25
  226.2 3.8 %collective-permute-start.26 = (f32[1,6,128]{2,1,0:T(8,128)S(1)}, f32[1,6,128]{2,1,0:T(8,128)S(1)}, u32[]{:S(2)}, u32[]{:S(2)}) collective-permute-start(f32[1,6,128]{2,1,0:T(8,128)S(1)} %bitcast_divide_fusion), channel_id=1, source_target_pairs={{0,1},{1,2},{2,3},{3,4},{4,5},{5,6},{6,7},{7,8},{8,9},{9,10},{10,1... | collective-permute-start | bytes 9224 | tf_op jit(solution)/shard_map/ppermute | solution.py:21
  230.0 3.5 %collective-permute-done.26 = f32[1,6,128]{2,1,0:T(8,128)S(1)} collective-permute-done((f32[1,6,128]{2,1,0:T(8,128)S(1)}, f32[1,6,128]{2,1,0:T(8,128)S(1)}, u32[]{:S(2)}, u32[]{:S(2)}) %collective-permute-start.26) | collective-permute-done | bytes 3104 | tf_op jit(solution)/shard_map/ppermute | solution.py:21
  235.5 3.9 %collective-permute-start.28 = (f32[1,6,128]{2,1,0:T(8,128)S(1)}, f32[1,6,128]{2,1,0:T(8,128)S(1)}, u32[]{:S(2)}, u32[]{:S(2)}) collective-permute-start(f32[1,6,128]{2,1,0:T(8,128)S(1)} %fusion.139), channel_id=1, source_target_pairs={{0,1},{1,2},{2,3},{3,4},{4,5},{5,6},{6,7},{7,8},{8,9},{9,10},{10,1... | collective-permute-start | bytes 9224 | tf_op jit(solution)/shard_map/ppermute | solution.py:21
  239.4 3.4 %collective-permute-done.28 = f32[1,6,128]{2,1,0:T(8,128)S(1)} collective-permute-done((f32[1,6,128]{2,1,0:T(8,128)S(1)}, f32[1,6,128]{2,1,0:T(8,128)S(1)}, u32[]{:S(2)}, u32[]{:S(2)}) %collective-permute-start.28) | collective-permute-done | bytes 3104 | tf_op jit(solution)/shard_map/ppermute | solution.py:21
  244.8 3.9 %collective-permute-start.30 = (f32[1,6,128]{2,1,0:T(8,128)S(1)}, f32[1,6,128]{2,1,0:T(8,128)S(1)}, u32[]{:S(2)}, u32[]{:S(2)}) collective-permute-start(f32[1,6,128]{2,1,0:T(8,128)S(1)} %fusion.150), channel_id=1, source_target_pairs={{0,1},{1,2},{2,3},{3,4},{4,5},{5,6},{6,7},{7,8},{8,9},{9,10},{10,1... | collective-permute-start | bytes 9224 | tf_op jit(solution)/shard_map/ppermute | solution.py:21
  248.7 3.4 %collective-permute-done.30 = f32[1,6,128]{2,1,0:T(8,128)S(1)} collective-permute-done((f32[1,6,128]{2,1,0:T(8,128)S(1)}, f32[1,6,128]{2,1,0:T(8,128)S(1)}, u32[]{:S(2)}, u32[]{:S(2)}) %collective-permute-start.30) | collective-permute-done | bytes 3104 | tf_op jit(solution)/shard_map/ppermute | solution.py:21
  (105 shorter events, 26.1 us)
Async XLA Ops:
  1.5 6.2 %collective-permute-start = (f32[1,24,512]{2,1,0:T(8,128)S(1)}, f32[1,24,512]{2,1,0:T(8,128)S(1)}, u32[]{:S(2)}, u32[]{:S(2)}) collective-permute-start(f32[1,24,512]{2,1,0:T(8,128)S(1)} %get-tuple-element.15), channel_id=1, source_target_pairs={{1,0},{2,1},{3,2},{4,3},{5,4},{6,5},{7,6},{8,7},{9,8},{10,9},{11,1... | collective-permute-start | bytes 147464 | tf_op jit(solution)/shard_map/ppermute | solution.py:24
  5.7 7.8 %collective-permute-start.1 = (f32[1,24,512]{2,1,0:T(8,128)S(1)}, f32[1,24,512]{2,1,0:T(8,128)S(1)}, u32[]{:S(2)}, u32[]{:S(2)}) collective-permute-start(f32[1,24,512]{2,1,0:T(8,128)S(1)} %get-tuple-element.16), channel_id=1, source_target_pairs={{0,1},{1,2},{2,3},{3,4},{4,5},{5,6},{6,7},{7,8},{8,9},{9,10},{10,1... | collective-permute-start | bytes 147464 | tf_op jit(solution)/shard_map/ppermute | solution.py:21
  15.4 46.6 %collective-permute-start.2 = (f32[1,24,512]{2,1,0:T(8,128)S(1)}, f32[1,24,512]{2,1,0:T(8,128)S(1)}, u32[]{:S(2)}, u32[]{:S(2)}) collective-permute-start(f32[1,24,512]{2,1,0:T(8,128)S(1)} %get-tuple-element.13), channel_id=1, source_target_pairs={{1,0},{2,1},{3,2},{4,3},{5,4},{6,5},{7,6},{8,7},{9,8},{10,9},{11,1... | collective-permute-start | bytes 147464 | tf_op jit(solution)/shard_map/ppermute | solution.py:24
  17.4 44.7 %collective-permute-start.3 = (f32[1,24,512]{2,1,0:T(8,128)S(1)}, f32[1,24,512]{2,1,0:T(8,128)S(1)}, u32[]{:S(2)}, u32[]{:S(2)}) collective-permute-start(f32[1,24,512]{2,1,0:T(8,128)S(1)} %get-tuple-element.14), channel_id=1, source_target_pairs={{0,1},{1,2},{2,3},{3,4},{4,5},{5,6},{6,7},{7,8},{8,9},{9,10},{10,1... | collective-permute-start | bytes 147464 | tf_op jit(solution)/shard_map/ppermute | solution.py:21
  40.7 21.4 %copy-start = (s32[4,24,512]{2,1,0:T(8,128)S(1)}, s32[4,24,512]{2,1,0:T(8,128)}, u32[]{:S(2)}) copy-start(s32[4,24,512]{2,1,0:T(8,128)} %param.7) | copy-start | bytes 589828
  40.7 21.3 %copy-start.1 = (f32[4,24,512]{2,1,0:T(8,128)S(1)}, f32[4,24,512]{2,1,0:T(8,128)}, u32[]{:S(2)}) copy-start(f32[4,24,512]{2,1,0:T(8,128)} %param.6) | copy-start | bytes 589828
  40.7 21.3 %copy-start.2 = (f32[1,2,4,24,512]{4,3,2,1,0:T(8,128)S(1)}, f32[1,2,4,24,512]{4,3,2,1,0:T(8,128)}, u32[]{:S(2)}) copy-start(f32[1,2,4,24,512]{4,3,2,1,0:T(8,128)} %param.5) | copy-start | bytes 1179652
  40.7 21.3 %copy-start.3 = (f32[1,4,24,512]{3,2,1,0:T(8,128)S(1)}, f32[1,4,24,512]{3,2,1,0:T(8,128)}, u32[]{:S(2)}) copy-start(f32[1,4,24,512]{3,2,1,0:T(8,128)} %param.4) | copy-start | bytes 589828
  82.6 5.9 %collective-permute-start.4 = (f32[1,6,128]{2,1,0:T(8,128)S(1)}, f32[1,6,128]{2,1,0:T(8,128)S(1)}, u32[]{:S(2)}, u32[]{:S(2)}) collective-permute-start(f32[1,6,128]{2,1,0:T(8,128)S(1)} %bitcast_divide_fusion.2), channel_id=1, source_target_pairs={{1,0},{2,1},{3,2},{4,3},{5,4},{6,5},{7,6},{8,7},{9,8},{10,9},{11,1... | collective-permute-start | bytes 9224 | tf_op jit(solution)/shard_map/ppermute | solution.py:24
  86.4 7.3 %collective-permute-start.5 = (f32[1,6,128]{2,1,0:T(8,128)S(1)}, f32[1,6,128]{2,1,0:T(8,128)S(1)}, u32[]{:S(2)}, u32[]{:S(2)}) collective-permute-start(f32[1,6,128]{2,1,0:T(8,128)S(1)} %bitcast_divide_fusion.2), channel_id=1, source_target_pairs={{0,1},{1,2},{2,3},{3,4},{4,5},{5,6},{6,7},{7,8},{8,9},{9,10},{10,1... | collective-permute-start | bytes 9224 | tf_op jit(solution)/shard_map/ppermute | solution.py:21
  93.7 5.9 %collective-permute-start.6 = (f32[1,6,128]{2,1,0:T(8,128)S(1)}, f32[1,6,128]{2,1,0:T(8,128)S(1)}, u32[]{:S(2)}, u32[]{:S(2)}) collective-permute-start(f32[1,6,128]{2,1,0:T(8,128)S(1)} %fusion.73), channel_id=1, source_target_pairs={{1,0},{2,1},{3,2},{4,3},{5,4},{6,5},{7,6},{8,7},{9,8},{10,9},{11,1... | collective-permute-start | bytes 9224 | tf_op jit(solution)/shard_map/ppermute | solution.py:24
  95.7 7.3 %collective-permute-start.7 = (f32[1,6,128]{2,1,0:T(8,128)S(1)}, f32[1,6,128]{2,1,0:T(8,128)S(1)}, u32[]{:S(2)}, u32[]{:S(2)}) collective-permute-start(f32[1,6,128]{2,1,0:T(8,128)S(1)} %fusion.73), channel_id=1, source_target_pairs={{0,1},{1,2},{2,3},{3,4},{4,5},{5,6},{6,7},{7,8},{8,9},{9,10},{10,1... | collective-permute-start | bytes 9224 | tf_op jit(solution)/shard_map/ppermute | solution.py:21
  103.0 5.9 %collective-permute-start.8 = (f32[1,6,128]{2,1,0:T(8,128)S(1)}, f32[1,6,128]{2,1,0:T(8,128)S(1)}, u32[]{:S(2)}, u32[]{:S(2)}) collective-permute-start(f32[1,6,128]{2,1,0:T(8,128)S(1)} %fusion.84), channel_id=1, source_target_pairs={{1,0},{2,1},{3,2},{4,3},{5,4},{6,5},{7,6},{8,7},{9,8},{10,9},{11,1... | collective-permute-start | bytes 9224 | tf_op jit(solution)/shard_map/ppermute | solution.py:24
  105.0 7.4 %collective-permute-start.9 = (f32[1,6,128]{2,1,0:T(8,128)S(1)}, f32[1,6,128]{2,1,0:T(8,128)S(1)}, u32[]{:S(2)}, u32[]{:S(2)}) collective-permute-start(f32[1,6,128]{2,1,0:T(8,128)S(1)} %fusion.84), channel_id=1, source_target_pairs={{0,1},{1,2},{2,3},{3,4},{4,5},{5,6},{6,7},{7,8},{8,9},{9,10},{10,1... | collective-permute-start | bytes 9224 | tf_op jit(solution)/shard_map/ppermute | solution.py:21
  113.1 6.0 %collective-permute-start.10 = (f32[1,24,512]{2,1,0:T(8,128)S(1)}, f32[1,24,512]{2,1,0:T(8,128)S(1)}, u32[]{:S(2)}, u32[]{:S(2)}) collective-permute-start(f32[1,24,512]{2,1,0:T(8,128)S(1)} %get-tuple-element.8), channel_id=1, source_target_pairs={{1,0},{2,1},{3,2},{4,3},{5,4},{6,5},{7,6},{8,7},{9,8},{10,9},{11,1... | collective-permute-start | bytes 147464 | tf_op jit(solution)/shard_map/ppermute | solution.py:24
  115.0 7.8 %collective-permute-start.11 = (f32[1,24,512]{2,1,0:T(8,128)S(1)}, f32[1,24,512]{2,1,0:T(8,128)S(1)}, u32[]{:S(2)}, u32[]{:S(2)}) collective-permute-start(f32[1,24,512]{2,1,0:T(8,128)S(1)} %get-tuple-element.9), channel_id=1, source_target_pairs={{0,1},{1,2},{2,3},{3,4},{4,5},{5,6},{6,7},{7,8},{8,9},{9,10},{10,1... | collective-permute-start | bytes 147464 | tf_op jit(solution)/shard_map/ppermute | solution.py:21
  123.0 6.0 %collective-permute-start.12 = (f32[1,24,512]{2,1,0:T(8,128)S(1)}, f32[1,24,512]{2,1,0:T(8,128)S(1)}, u32[]{:S(2)}, u32[]{:S(2)}) collective-permute-start(f32[1,24,512]{2,1,0:T(8,128)S(1)} %get-tuple-element.6), channel_id=1, source_target_pairs={{1,0},{2,1},{3,2},{4,3},{5,4},{6,5},{7,6},{8,7},{9,8},{10,9},{11,1... | collective-permute-start | bytes 147464 | tf_op jit(solution)/shard_map/ppermute | solution.py:24
  125.2 7.8 %collective-permute-start.13 = (f32[1,24,512]{2,1,0:T(8,128)S(1)}, f32[1,24,512]{2,1,0:T(8,128)S(1)}, u32[]{:S(2)}, u32[]{:S(2)}) collective-permute-start(f32[1,24,512]{2,1,0:T(8,128)S(1)} %get-tuple-element.7), channel_id=1, source_target_pairs={{0,1},{1,2},{2,3},{3,4},{4,5},{5,6},{6,7},{7,8},{8,9},{9,10},{10,1... | collective-permute-start | bytes 147464 | tf_op jit(solution)/shard_map/ppermute | solution.py:21
  153.5 5.9 %collective-permute-start.14 = (f32[1,6,128]{2,1,0:T(8,128)S(1)}, f32[1,6,128]{2,1,0:T(8,128)S(1)}, u32[]{:S(2)}, u32[]{:S(2)}) collective-permute-start(f32[1,6,128]{2,1,0:T(8,128)S(1)} %bitcast_divide_fusion.1), channel_id=1, source_target_pairs={{1,0},{2,1},{3,2},{4,3},{5,4},{6,5},{7,6},{8,7},{9,8},{10,9},{11,1... | collective-permute-start | bytes 9224 | tf_op jit(solution)/shard_map/ppermute | solution.py:24
  155.5 7.3 %collective-permute-start.15 = (f32[1,6,128]{2,1,0:T(8,128)S(1)}, f32[1,6,128]{2,1,0:T(8,128)S(1)}, u32[]{:S(2)}, u32[]{:S(2)}) collective-permute-start(f32[1,6,128]{2,1,0:T(8,128)S(1)} %bitcast_divide_fusion.1), channel_id=1, source_target_pairs={{0,1},{1,2},{2,3},{3,4},{4,5},{5,6},{6,7},{7,8},{8,9},{9,10},{10,1... | collective-permute-start | bytes 9224 | tf_op jit(solution)/shard_map/ppermute | solution.py:21
  162.8 5.9 %collective-permute-start.16 = (f32[1,6,128]{2,1,0:T(8,128)S(1)}, f32[1,6,128]{2,1,0:T(8,128)S(1)}, u32[]{:S(2)}, u32[]{:S(2)}) collective-permute-start(f32[1,6,128]{2,1,0:T(8,128)S(1)} %fusion.106), channel_id=1, source_target_pairs={{1,0},{2,1},{3,2},{4,3},{5,4},{6,5},{7,6},{8,7},{9,8},{10,9},{11,1... | collective-permute-start | bytes 9224 | tf_op jit(solution)/shard_map/ppermute | solution.py:24
  164.9 7.3 %collective-permute-start.17 = (f32[1,6,128]{2,1,0:T(8,128)S(1)}, f32[1,6,128]{2,1,0:T(8,128)S(1)}, u32[]{:S(2)}, u32[]{:S(2)}) collective-permute-start(f32[1,6,128]{2,1,0:T(8,128)S(1)} %fusion.106), channel_id=1, source_target_pairs={{0,1},{1,2},{2,3},{3,4},{4,5},{5,6},{6,7},{7,8},{8,9},{9,10},{10,1... | collective-permute-start | bytes 9224 | tf_op jit(solution)/shard_map/ppermute | solution.py:21
  172.3 5.9 %collective-permute-start.18 = (f32[1,6,128]{2,1,0:T(8,128)S(1)}, f32[1,6,128]{2,1,0:T(8,128)S(1)}, u32[]{:S(2)}, u32[]{:S(2)}) collective-permute-start(f32[1,6,128]{2,1,0:T(8,128)S(1)} %fusion.117), channel_id=1, source_target_pairs={{1,0},{2,1},{3,2},{4,3},{5,4},{6,5},{7,6},{8,7},{9,8},{10,9},{11,1... | collective-permute-start | bytes 9224 | tf_op jit(solution)/shard_map/ppermute | solution.py:24
  174.2 7.3 %collective-permute-start.19 = (f32[1,6,128]{2,1,0:T(8,128)S(1)}, f32[1,6,128]{2,1,0:T(8,128)S(1)}, u32[]{:S(2)}, u32[]{:S(2)}) collective-permute-start(f32[1,6,128]{2,1,0:T(8,128)S(1)} %fusion.117), channel_id=1, source_target_pairs={{0,1},{1,2},{2,3},{3,4},{4,5},{5,6},{6,7},{7,8},{8,9},{9,10},{10,1... | collective-permute-start | bytes 9224 | tf_op jit(solution)/shard_map/ppermute | solution.py:21
  182.2 1.5 collective-permute-start.20
  183.7 6.0 %collective-permute-start.21 = (f32[1,24,512]{2,1,0:T(8,128)S(1)}, f32[1,24,512]{2,1,0:T(8,128)S(1)}, u32[]{:S(2)}, u32[]{:S(2)}) collective-permute-start(f32[1,24,512]{2,1,0:T(8,128)S(1)} %get-tuple-element.4), channel_id=1, source_target_pairs={{1,0},{2,1},{3,2},{4,3},{5,4},{6,5},{7,6},{8,7},{9,8},{10,9},{11,1... | collective-permute-start | bytes 147464 | tf_op jit(solution)/shard_map/ppermute | solution.py:24
  185.8 7.8 %collective-permute-start.22 = (f32[1,24,512]{2,1,0:T(8,128)S(1)}, f32[1,24,512]{2,1,0:T(8,128)S(1)}, u32[]{:S(2)}, u32[]{:S(2)}) collective-permute-start(f32[1,24,512]{2,1,0:T(8,128)S(1)} %get-tuple-element.5), channel_id=1, source_target_pairs={{0,1},{1,2},{2,3},{3,4},{4,5},{5,6},{6,7},{7,8},{8,9},{9,10},{10,1... | collective-permute-start | bytes 147464 | tf_op jit(solution)/shard_map/ppermute | solution.py:21
  193.9 6.2 %collective-permute-start.23 = (f32[1,24,512]{2,1,0:T(8,128)S(1)}, f32[1,24,512]{2,1,0:T(8,128)S(1)}, u32[]{:S(2)}, u32[]{:S(2)}) collective-permute-start(f32[1,24,512]{2,1,0:T(8,128)S(1)} %get-tuple-element.2), channel_id=1, source_target_pairs={{1,0},{2,1},{3,2},{4,3},{5,4},{6,5},{7,6},{8,7},{9,8},{10,9},{11,1... | collective-permute-start | bytes 147464 | tf_op jit(solution)/shard_map/ppermute | solution.py:24
  195.8 7.8 %collective-permute-start.24 = (f32[1,24,512]{2,1,0:T(8,128)S(1)}, f32[1,24,512]{2,1,0:T(8,128)S(1)}, u32[]{:S(2)}, u32[]{:S(2)}) collective-permute-start(f32[1,24,512]{2,1,0:T(8,128)S(1)} %get-tuple-element.3), channel_id=1, source_target_pairs={{0,1},{1,2},{2,3},{3,4},{4,5},{5,6},{6,7},{7,8},{8,9},{9,10},{10,1... | collective-permute-start | bytes 147464 | tf_op jit(solution)/shard_map/ppermute | solution.py:21
  224.1 5.9 %collective-permute-start.25 = (f32[1,6,128]{2,1,0:T(8,128)S(1)}, f32[1,6,128]{2,1,0:T(8,128)S(1)}, u32[]{:S(2)}, u32[]{:S(2)}) collective-permute-start(f32[1,6,128]{2,1,0:T(8,128)S(1)} %bitcast_divide_fusion), channel_id=1, source_target_pairs={{1,0},{2,1},{3,2},{4,3},{5,4},{6,5},{7,6},{8,7},{9,8},{10,9},{11,1... | collective-permute-start | bytes 9224 | tf_op jit(solution)/shard_map/ppermute | solution.py:24
  226.2 7.3 %collective-permute-start.26 = (f32[1,6,128]{2,1,0:T(8,128)S(1)}, f32[1,6,128]{2,1,0:T(8,128)S(1)}, u32[]{:S(2)}, u32[]{:S(2)}) collective-permute-start(f32[1,6,128]{2,1,0:T(8,128)S(1)} %bitcast_divide_fusion), channel_id=1, source_target_pairs={{0,1},{1,2},{2,3},{3,4},{4,5},{5,6},{6,7},{7,8},{8,9},{9,10},{10,1... | collective-permute-start | bytes 9224 | tf_op jit(solution)/shard_map/ppermute | solution.py:21
  233.6 5.9 %collective-permute-start.27 = (f32[1,6,128]{2,1,0:T(8,128)S(1)}, f32[1,6,128]{2,1,0:T(8,128)S(1)}, u32[]{:S(2)}, u32[]{:S(2)}) collective-permute-start(f32[1,6,128]{2,1,0:T(8,128)S(1)} %fusion.139), channel_id=1, source_target_pairs={{1,0},{2,1},{3,2},{4,3},{5,4},{6,5},{7,6},{8,7},{9,8},{10,9},{11,1... | collective-permute-start | bytes 9224 | tf_op jit(solution)/shard_map/ppermute | solution.py:24
  235.5 7.3 %collective-permute-start.28 = (f32[1,6,128]{2,1,0:T(8,128)S(1)}, f32[1,6,128]{2,1,0:T(8,128)S(1)}, u32[]{:S(2)}, u32[]{:S(2)}) collective-permute-start(f32[1,6,128]{2,1,0:T(8,128)S(1)} %fusion.139), channel_id=1, source_target_pairs={{0,1},{1,2},{2,3},{3,4},{4,5},{5,6},{6,7},{7,8},{8,9},{9,10},{10,1... | collective-permute-start | bytes 9224 | tf_op jit(solution)/shard_map/ppermute | solution.py:21
  242.9 5.9 %collective-permute-start.29 = (f32[1,6,128]{2,1,0:T(8,128)S(1)}, f32[1,6,128]{2,1,0:T(8,128)S(1)}, u32[]{:S(2)}, u32[]{:S(2)}) collective-permute-start(f32[1,6,128]{2,1,0:T(8,128)S(1)} %fusion.150), channel_id=1, source_target_pairs={{1,0},{2,1},{3,2},{4,3},{5,4},{6,5},{7,6},{8,7},{9,8},{10,9},{11,1... | collective-permute-start | bytes 9224 | tf_op jit(solution)/shard_map/ppermute | solution.py:24
  244.8 7.3 %collective-permute-start.30 = (f32[1,6,128]{2,1,0:T(8,128)S(1)}, f32[1,6,128]{2,1,0:T(8,128)S(1)}, u32[]{:S(2)}, u32[]{:S(2)}) collective-permute-start(f32[1,6,128]{2,1,0:T(8,128)S(1)} %fusion.150), channel_id=1, source_target_pairs={{0,1},{1,2},{2,3},{3,4},{4,5},{5,6},{6,7},{7,8},{8,9},{9,10},{10,1... | collective-permute-start | bytes 9224 | tf_op jit(solution)/shard_map/ppermute | solution.py:21
where the time goes:
time: 255 us; the launch traced here: 254 us
  starting transfers between devices  88.2 us (35%)
  local copies, waits for them, and re-layouts  76.5 us (30%)
  waiting for transfers between devices  55.3 us (22%)
  other arithmetic  32.9 us (13%)
    reshape x5, local copies, waits for them, and re-layouts, shrink(): return field.reshape(a // 2, 2, b // 2, 2, c // 2, 2).mean(axis=(1, 3, 5))  69.4 us
    ppermute x15, starting transfers between devices, padded(): lax.ppermute(lax.slice_in_dim(block, block.shape[dim] - width, None, axis...  54.6 us
    ppermute x15, waiting for transfers between devices, padded(): lax.ppermute(lax.slice_in_dim(block, block.shape[dim] - width, None, axis...  53.2 us
    ppermute x15, starting transfers between devices, padded(): lax.ppermute(lax.slice_in_dim(block, 0, width, axis=dim), axis, backward)  33.5 us
    reduce_sum x15, other arithmetic, shrink(): return field.reshape(a // 2, 2, b // 2, 2, c // 2, 2).mean(axis=(1, 3, 5))  28.4 us
  transfers between devices with their start and end apart: 31, of which 18 were waited for; matrix products, arithmetic and copies ran while one was open for 16% of the time, Pallas kernels for 0%

commit v1 on v0

v1 whole, which is shorter than its diff:
```python
import functools

import jax
import jax.numpy as jnp
from jax import lax
from jax.experimental import pallas as pl
from jax.experimental.pallas import tpu as pltpu
from jax.sharding import PartitionSpec as P

COARSE_SWEEPS = 4
STIFFNESS = 4.0
COARSE_STIFF = 0.25
FORCE_WEIGHT = 0.5
RELAX = 0.8
MASS_FLAG = 3.0

MESH = pl.DeviceIdType.MESH
REACH = COARSE_SWEEPS
SLOTS = 2 * REACH + 1
F32 = jnp.float32
BF16 = jnp.bfloat16


def pieces(x):
    hi = x.astype(BF16).astype(F32)
    rest = x - hi
    mid = rest.astype(BF16).astype(F32)
    low = (rest - mid).astype(BF16).astype(F32)
    return [hi, mid, low]


def kernel(
    n, nt, planes,
    starts, forcing, density, flags, out_starts, out_interior,
    prior, state, came, force, rho, moving, stiff, diag, beta,
    ring, own, gam, rows, wide, narrow, spread, final,
    load_sem, send_sem, recv_sem,
):
    t = lax.axis_index("tm")
    me = lax.axis_index("space")
    ahead, behind = lax.rem(t + 1, nt), lax.rem(t + nt - 1, nt)
    top = planes + 1
    ny, nz = prior.shape[-2:]
    ncy, ncz = 8, nz // 4

    def inside(offset):
        if offset < 0:
            return me >= -offset
        return me < n - offset

    offsets = [d for d in range(-REACH, REACH + 1)]

    barrier = pltpu.get_barrier_semaphore()
    for d in (1, -1, 2, -2, 3, -3, 4, -4):
        @pl.when(inside(d))
        def _(d=d):
            pl.semaphore_signal(barrier, inc=1, device_id=(t, me + d), device_id_type=MESH)
            pl.semaphore_signal(barrier, inc=1, device_id=(behind, me + d), device_id_type=MESH)
    pl.semaphore_signal(barrier, inc=1, device_id=(behind, me), device_id_type=MESH)

    loads = [
        pltpu.make_async_copy(density, rho, load_sem.at[0]),
        pltpu.make_async_copy(flags, moving, load_sem.at[1]),
        pltpu.make_async_copy(starts.at[0], prior.at[0, pl.ds(1, planes)], load_sem.at[2]),
        pltpu.make_async_copy(forcing.at[0], force, load_sem.at[3]),
    ]
    for load in loads:
        load.start()

    sends = []

    def copy_to(src, dst, k, device):
        return pltpu.make_async_remote_copy(
            src_ref=src, dst_ref=dst, send_sem=send_sem.at[k], recv_sem=recv_sem.at[k],
            device_id=device, device_id_type=MESH,
        )

    def send(src, dst, k, offset, tm):
        copy = copy_to(src, dst, k, (tm, me + offset))
        if offset == 0:
            copy.start()
        else:
            pl.when(inside(offset))(lambda: copy.start())
        sends.append((copy, offset))

    def receive(dst, k, offset):
        copy = copy_to(dst, dst, k, (t, me))
        if offset == 0:
            copy.wait_recv()
        else:
            pl.when(inside(offset))(lambda: copy.wait_recv())

    for d in offsets:
        if d == 0:
            continue

        @pl.when(jnp.logical_not(inside(d)))
        def _(d=d):
            zero = jnp.zeros(ring.shape[2:], F32)
            gam[REACH + d] = zero
            for step in range(3):
                ring[step, REACH + d] = zero
            if abs(d) == 1:
                plane = 0 if d < 0 else top
                fine_zero = jnp.zeros((ny, nz), F32)
                prior[0, plane] = fine_zero
                for step in range(3):
                    state[step, plane] = fine_zero

    narrow[...] = (
        lax.broadcasted_iota(jnp.int32, (nz, ncz), 0) // 4 == lax.broadcasted_iota(jnp.int32, (nz, ncz), 1)
    ).astype(F32).astype(BF16)
    one = (
        lax.broadcasted_iota(jnp.int32, (ncz, nz), 1) // 4 == lax.broadcasted_iota(jnp.int32, (ncz, nz), 0)
    ).astype(F32).astype(BF16)
    for piece in range(3):
        wide[pl.ds(piece * ncz, ncz), :] = one
    rows[...] = jnp.zeros_like(rows)

    row = lax.broadcasted_iota(jnp.int32, (ny, nz), 0)
    lane = lax.broadcasted_iota(jnp.int32, (ny, nz), 1)

    def beside(x):
        up = jnp.where(row == 0, 0.0, pltpu.roll(x, 1, 0))
        down = jnp.where(row == ny - 1, 0.0, pltpu.roll(x, ny - 1, 0))
        left = jnp.where(lane == 0, 0.0, pltpu.roll(x, 1, 1))
        right = jnp.where(lane == nz - 1, 0.0, pltpu.roll(x, nz - 1, 1))
        return (up + down) + (left + right)

    clane = lax.broadcasted_iota(jnp.int32, (ncy, ncz), 1)

    def coarse_beside(x):
        left = jnp.where(clane == 0, 0.0, pltpu.roll(x, 1, 1))
        right = jnp.where(clane == ncz - 1, 0.0, pltpu.roll(x, ncz - 1, 1))
        return (pltpu.roll(x, 1, 0) + pltpu.roll(x, ncy - 1, 0)) + (left + right)

    def coarsen(total, slot):
        stacked = jnp.concatenate(pieces(total), axis=0).astype(BF16)
        product = jnp.dot(stacked, narrow[...], preferred_element_type=F32)
        rows[slot, pl.ds(0, ny), :] = (product[:ny] + product[ny:2 * ny]) + product[2 * ny:]
        parts = [rows[slot, pl.ds(k, ncy, stride=4), :] for k in range(4)]
        return ((parts[0] + parts[1]) + (parts[2] + parts[3])) * (1.0 / 64.0)

    for load in loads[:2]:
        load.wait()
    mass_sum = jnp.zeros((ny, nz), F32)
    conduct_sum = jnp.zeros((ny, nz), F32)
    for k in range(planes):
        conduct = 1.0 / rho[k]
        mass = 1.0 + MASS_FLAG * moving[k].astype(F32)
        full = mass + 6.0 * STIFFNESS * conduct
        stiff[k] = STIFFNESS * conduct
        diag[k] = full
        beta[k] = RELAX / full
        mass_sum = mass_sum + mass
        conduct_sum = conduct_sum + conduct

    pl.semaphore_wait(barrier, 1 + 2 * sum(inside(d).astype(jnp.int32) for d in offsets if d != 0))
    send(starts.at[0, 0], prior.at[0, top], 1, -1, t)
    send(starts.at[0, planes - 1], prior.at[0, 0], 0, 1, t)

    mass_c = coarsen(mass_sum, 0)
    conduct_c = coarsen(conduct_sum, 1)
    real = lax.broadcasted_iota(jnp.int32, (ncy, ncz), 0) < ny // 4
    relax_c = jnp.where(real, RELAX / jnp.where(real, mass_c + 6.0 * COARSE_STIFF * conduct_c, 1.0), 0.0)
    gam[REACH] = COARSE_STIFF * conduct_c * relax_c
    for d in offsets:
        if d != 0:
            send(gam.at[REACH], gam.at[REACH - d], 20 + REACH - d, d, t)
    for load in loads[2:]:
        load.wait()

    def smooth(step, k):
        source = force[step % 2, k]
        here = prior[step, k + 1]
        around = beside(here) + (prior[step, k] + prior[step, k + 2])
        state[step, k + 1] = here + beta[k] * (FORCE_WEIGHT * source - stiff[k] * (6.0 * here - around))

    def residual(step):
        total = jnp.zeros((ny, nz), F32)
        for k in range(planes):
            full, mine = diag[k], state[step, k + 1]
            mass = full - 6.0 * stiff[k]
            around = beside(mine)
            if k > 0:
                around = around + state[step, k]
            if k < planes - 1:
                around = around + state[step, k + 2]
            total = total + (mass * prior[step, k + 1] + FORCE_WEIGHT * force[step % 2, k]) - (full * mine - stiff[k] * around)
        return total

    def solve(step, width):
        right = {i: ring[step, i] for i in range(1 - width, SLOTS - 1 + width)}
        error = right
        for sweep in range(COARSE_SWEEPS - 1):
            reach = COARSE_SWEEPS - 2 - sweep + width
            error = {
                i: (1.0 - RELAX) * error[i] + right[i]
                + gam[i] * (coarse_beside(error[i]) + (error[i - 1] + error[i + 1]))
                for i in range(REACH - reach, REACH + reach + 1)
            }
        return [error[i] for i in range(REACH - width, REACH + width + 1)]

    def expanded(errors):
        for j, error in enumerate(errors):
            for k in range(4):
                spread[j, pl.ds(k, ncy, stride=4), :] = error
        tall = jnp.concatenate([spread[j, pl.ds(0, ny), :] for j in range(len(errors))], axis=0)
        stacked = jnp.concatenate(pieces(tall), axis=1).astype(BF16)
        product = jnp.dot(stacked, wide[...], preferred_element_type=F32)
        return [product[j * ny:(j + 1) * ny] for j in range(len(errors))]

    def exchange(step):
        send(state.at[step, 1], state.at[step, top], 3 + 2 * step, -1, t)

    for step in range(3):
        low, high = 2 + 2 * step, 3 + 2 * step
        if step == 0:
            for k in range(1, planes - 1):
                smooth(step, k)
            receive(prior.at[0, 0], 0, -1)
            smooth(step, 0)
            send(state.at[step, 1], state.at[step, top], high, -1, t)
            receive(prior.at[0, top], 1, 1)
            smooth(step, planes - 1)
            send(state.at[step, planes], state.at[step, 0], low, 1, t)
        else:
            smooth(step, 0)
            send(state.at[step, 1], state.at[step, top], high, -1, t)
            smooth(step, planes - 1)
            send(state.at[step, planes], state.at[step, 0], low, 1, t)
            for k in range(1, planes - 1):
                smooth(step, k)
        if step == 1:
            send(state.at[step, pl.ds(1, planes)], came.at[pl.ds(1, planes)], 8, 0, ahead)
        total = residual(step)
        receive(state.at[step, 0], low, -1)
        receive(state.at[step, top], high, 1)
        total = total + stiff[0] * state[step, 0] + stiff[planes - 1] * state[step, top]
        right = relax_c * coarsen(total, step % 2)
        if step == 1:
            own[...] = right
            for d in offsets:
                send(own, ring.at[step, REACH - d], 40 + REACH - d, d, ahead)
            send(state.at[step, 0], came.at[0], 9, 0, ahead)
            send(state.at[step, top], came.at[top], 10, 0, ahead)
        else:
            ring[step, REACH] = right
            for d in offsets:
                if d != 0 and (step == 0 or abs(d) < REACH):
                    send(ring.at[step, REACH], ring.at[step, REACH - d], 30 + 10 * step + REACH - d, d, t)
        if step == 0:
            for d in offsets:
                if d != 0:
                    receive(gam.at[REACH + d], 20 + REACH + d, d)
        for d in offsets:
            if (d != 0 or step == 1) and (step < 2 or abs(d) < REACH):
                receive(ring.at[step, REACH + d], 30 + 10 * step + REACH + d, d)
        if step < 2:
            corrections = expanded(solve(step, 1))
            if step == 1:
                receive(came.at[pl.ds(1, planes)], 8, 0)
                receive(came.at[0], 9, 0)
                receive(came.at[top], 10, 0)
            for k in range(planes + 2):
                which = 0 if k == 0 else 2 if k == top else 1
                base = state[0, k] if step == 0 else came[k]
                prior[step + 1, k] = base + corrections[which]
            if step == 1:
                done = pltpu.make_async_copy(prior.at[2, pl.ds(1, planes)], out_starts.at[0], load_sem.at[4])
                done.start()
        else:
            correction = expanded(solve(step, 0))[0]
            for k in range(planes):
                final[k] = state[2, k + 1] + correction
    last = pltpu.make_async_copy(final, out_interior.at[0], load_sem.at[5])
    last.start()
    for copy, offset in sends:
        if offset == 0:
            copy.wait_send()
        else:
            pl.when(inside(offset))(lambda copy=copy: copy.wait_send())
    done.wait()
    last.wait()


def solution(mesh):
    n, nt = mesh.shape["space"], mesh.shape["tm"]

    def local(slab_starts, forcing, density, moving_flags):
        _, planes, ny, nz = slab_starts.shape
        block = (planes, ny, nz)
        coarse = (8, nz // 4)
        result = jax.ShapeDtypeStruct(slab_starts.shape, F32)
        return pl.pallas_call(
            functools.partial(kernel, n, nt, planes),
            out_shape=(result, result),
            in_specs=[pl.BlockSpec(memory_space=pl.ANY)] * 4,
            out_specs=(pl.BlockSpec(memory_space=pl.ANY),) * 2,
            scratch_shapes=[
                pltpu.VMEM((3, planes + 2, ny, nz), F32),
                pltpu.VMEM((3, planes + 2, ny, nz), F32),
                pltpu.VMEM((planes + 2, ny, nz), F32),
                pltpu.VMEM((2,) + block, F32),
                pltpu.VMEM(block, F32),
                pltpu.VMEM(block, jnp.int32),
                pltpu.VMEM(block, F32),
                pltpu.VMEM(block, F32),
                pltpu.VMEM(block, F32),
                pltpu.VMEM((3, SLOTS) + coarse, F32),
                pltpu.VMEM(coarse, F32),
                pltpu.VMEM((SLOTS,) + coarse, F32),
                pltpu.VMEM((2, 32, nz // 4), F32),
                pltpu.VMEM((3 * nz // 4, nz), BF16),
                pltpu.VMEM((nz, nz // 4), BF16),
                pltpu.VMEM((3, 32, nz // 4), F32),
                pltpu.VMEM(block, F32),
                pltpu.SemaphoreType.DMA((6,)),
                pltpu.SemaphoreType.DMA((60,)),
                pltpu.SemaphoreType.DMA((60,)),
            ],
            compiler_params=pltpu.CompilerParams(
                collective_id=0, has_side_effects=True, vmem_limit_bytes=32 * 1024 * 1024
            ),
            name="cycle",
        )(slab_starts, forcing, density, moving_flags)

    placed = (
        P("tm", "space", None, None),
        P("tm", None, "space", None, None),
        P("space", None, None),
        P("space", None, None),
    )
    return jax.shard_map(
        local,
        mesh=mesh,
        in_specs=placed,
        out_specs=(P("tm", "space", None, None), P("tm", "space", None, None)),
        check_vma=False,
    )
```

time: 255 us -> 38.5 us (0.15)
  the two profiles are of different devices: /device:TPU:24 before, /device:TPU:1 now
where the time goes in v1:
time: 38.5 us; the launch traced here: 38.2 us
  Pallas kernels  32.5 us (84%)
  local copies, waits for them, and re-layouts  5.12 us (13%)
  between operations  0.65 us (2%)
    pallas_call x1, Pallas kernels, local(): pl.pallas_call(functools.partial(kernel, n, nt, planes), out_shape=(resul...  32.5 us
    unnamed x10, local copies, waits for them, and re-layouts  5.12 us

profile of v1, /device:TPU:1, one launch (start us, length us, event | category | flops | bytes accessed | tf_op | source)
XLA Modules:
  0.0 38.2 jit_solution(4422928339300335560)
XLA Ops:
  0.6 0.0 copy-start
  0.6 1.0 %copy-done = f32[1,2,4,24,512]{4,3,2,1,0:T(8,128)S(1)} copy-done((f32[1,2,4,24,512]{4,3,2,1,0:T(8,128)S(1)}, f32[1,2,4,24,512]{4,3,2,1,0:T(8,128)}, u32[]{:S(2)}) %copy-start) | copy-done | bytes 393240
  1.6 0.0 copy-start.1
  1.6 0.9 %copy-done.1 = f32[1,4,24,512]{3,2,1,0:T(8,128)S(1)} copy-done((f32[1,4,24,512]{3,2,1,0:T(8,128)S(1)}, f32[1,4,24,512]{3,2,1,0:T(8,128)}, u32[]{:S(2)}) %copy-start.1) | copy-done | bytes 196632
  2.6 0.0 copy-start.2
  2.6 0.9 %copy-done.2 = f32[4,24,512]{2,1,0:T(8,128)S(1)} copy-done((f32[4,24,512]{2,1,0:T(8,128)S(1)}, f32[4,24,512]{2,1,0:T(8,128)}, u32[]{:S(2)}) %copy-start.2) | copy-done | bytes 196632
  3.5 0.0 copy-start.3
  3.5 0.9 %copy-done.3 = s32[4,24,512]{2,1,0:T(8,128)S(1)} copy-done((s32[4,24,512]{2,1,0:T(8,128)S(1)}, s32[4,24,512]{2,1,0:T(8,128)}, u32[]{:S(2)}) %copy-start.3) | copy-done | bytes 196632
  4.4 32.5 %cycle.1 = (f32[1,4,24,512]{3,2,1,0:T(8,128)S(1)}, f32[1,4,24,512]{3,2,1,0:T(8,128)S(1)}) custom-call(f32[1,4,24,512]{3,2,1,0:T(8,128)S(1)} %copy-done.1, f32[1,2,4,24,512]{4,3,2,1,0:T(8,128)S(1)} %copy-done, f32[4,24,512]{2,1,0:T(8,128)S(1)} %copy-done.2, s32[4,24,512]{2,1,0:T(8,128)S(1)} %copy-done.3), custom_call_target="tpu_custom_call" | custom-call | tf_op jit(solution)/shard_map/cycle/pallas_call | solution.py:295
  36.9 0.7 %copy.8 = f32[1,4,24,512]{3,2,1,0:T(8,128)} copy(f32[1,4,24,512]{3,2,1,0:T(8,128)S(1)} %get-tuple-element.4) | data formatting | bytes 393216
  37.6 0.7 %copy.9 = f32[1,4,24,512]{3,2,1,0:T(8,128)} copy(f32[1,4,24,512]{3,2,1,0:T(8,128)S(1)} %get-tuple-element.5) | data formatting | bytes 393216
Async XLA Ops:
  0.6 1.0 %copy-start = (f32[1,2,4,24,512]{4,3,2,1,0:T(8,128)S(1)}, f32[1,2,4,24,512]{4,3,2,1,0:T(8,128)}, u32[]{:S(2)}) copy-start(f32[1,2,4,24,512]{4,3,2,1,0:T(8,128)} %forcing.1) | copy-start | bytes 1179652
  1.6 0.9 %copy-start.1 = (f32[1,4,24,512]{3,2,1,0:T(8,128)S(1)}, f32[1,4,24,512]{3,2,1,0:T(8,128)}, u32[]{:S(2)}) copy-start(f32[1,4,24,512]{3,2,1,0:T(8,128)} %starts.1) | copy-start | bytes 589828
  2.6 0.9 %copy-start.2 = (f32[4,24,512]{2,1,0:T(8,128)S(1)}, f32[4,24,512]{2,1,0:T(8,128)}, u32[]{:S(2)}) copy-start(f32[4,24,512]{2,1,0:T(8,128)} %density.1) | copy-start | bytes 589828
  3.5 0.9 %copy-start.3 = (s32[4,24,512]{2,1,0:T(8,128)S(1)}, s32[4,24,512]{2,1,0:T(8,128)}, u32[]{:S(2)}) copy-start(s32[4,24,512]{2,1,0:T(8,128)} %flags.1) | copy-start | bytes 589828

commit v2 on v1

--- a/solution.py
+++ b/solution.py
@@ -32,14 +32,14 @@
 def kernel(
     n, nt, planes,
     starts, forcing, density, flags, out_starts, out_interior,
-    prior, state, came, force, rho, moving, stiff, diag, beta,
+    prior, state, came, force, rho, moving, stiff, diag, alpha, beta, local_part,
     ring, own, gam, rows, wide, narrow, spread, final,
     load_sem, send_sem, recv_sem,
 ):
     t = lax.axis_index("tm")
     me = lax.axis_index("space")
     ahead, behind = lax.rem(t + 1, nt), lax.rem(t + nt - 1, nt)
-    top = planes + 1
+    top = planes + 2
     ny, nz = prior.shape[-2:]
     ncy, ncz = 8, nz // 4
 
@@ -61,7 +61,7 @@
     loads = [
         pltpu.make_async_copy(density, rho, load_sem.at[0]),
         pltpu.make_async_copy(flags, moving, load_sem.at[1]),
-        pltpu.make_async_copy(starts.at[0], prior.at[0, pl.ds(1, planes)], load_sem.at[2]),
+        pltpu.make_async_copy(starts.at[0], prior.at[0, pl.ds(2, planes)], load_sem.at[2]),
         pltpu.make_async_copy(forcing.at[0], force, load_sem.at[3]),
     ]
     for load in loads:
@@ -101,11 +101,15 @@
             for step in range(3):
                 ring[step, REACH + d] = zero
             if abs(d) == 1:
-                plane = 0 if d < 0 else top
+                side = 0 if d < 0 else 1
                 fine_zero = jnp.zeros((ny, nz), F32)
-                prior[0, plane] = fine_zero
-                for step in range(3):
-                    state[step, plane] = fine_zero
+                prior[0, 1 if d < 0 else top] = fine_zero
+                local_part[side] = fine_zero
+                beta[side * (planes + 1)] = fine_zero
+                alpha[0, side * (planes + 1)] = fine_zero
+                alpha[1, side * (planes + 1)] = fine_zero
+                state[0, side * (top + 1)] = fine_zero
+                came[side * (top + 1)] = fine_zero
 
     narrow[...] = (
         lax.broadcasted_iota(jnp.int32, (nz, ncz), 0) // 4 == lax.broadcasted_iota(jnp.int32, (nz, ncz), 1)
@@ -141,23 +145,48 @@
         parts = [rows[slot, pl.ds(k, ncy, stride=4), :] for k in range(4)]
         return ((parts[0] + parts[1]) + (parts[2] + parts[3])) * (1.0 / 64.0)
 
-    for load in loads[:2]:
+    pl.semaphore_wait(barrier, 1 + 2 * sum(inside(d).astype(jnp.int32) for d in offsets if d != 0))
+    send(starts.at[0, 0], prior.at[0, top], 1, -1, t)
+    send(starts.at[0, planes - 1], prior.at[0, 1], 0, 1, t)
+
+    for load in loads:
         load.wait()
-    mass_sum = jnp.zeros((ny, nz), F32)
-    conduct_sum = jnp.zeros((ny, nz), F32)
-    for k in range(planes):
+
+    def coefficients(k):
         conduct = 1.0 / rho[k]
         mass = 1.0 + MASS_FLAG * moving[k].astype(F32)
         full = mass + 6.0 * STIFFNESS * conduct
+        relax = RELAX / full
         stiff[k] = STIFFNESS * conduct
         diag[k] = full
-        beta[k] = RELAX / full
-        mass_sum = mass_sum + mass
-        conduct_sum = conduct_sum + conduct
-
-    pl.semaphore_wait(barrier, 1 + 2 * sum(inside(d).astype(jnp.int32) for d in offsets if d != 0))
-    send(starts.at[0, 0], prior.at[0, top], 1, -1, t)
-    send(starts.at[0, planes - 1], prior.at[0, 0], 0, 1, t)
+        beta[k + 1] = (STIFFNESS * conduct) * relax
+        for step in range(2):
+            alpha[step, k + 1] = (FORCE_WEIGHT * force[step, k]) * relax
+        return mass, conduct
+
+    def smooth(step, i, below=True, above=True):
+        here = prior[step, i]
+        around = beside(here)
+        if below:
+            around = around + prior[step, i - 1]
+        if above:
+            around = around + prior[step, i + 1]
+        return here + (alpha[step % 2, i - 1] + beta[i - 1] * (around - 6.0 * here))
+
+    sums = [coefficients(0)]
+    send(beta.at[1], beta.at[planes + 1], 3, -1, t)
+    part_low = smooth(0, 2, below=False)
+    local_part[2] = part_low
+    send(local_part.at[2], local_part.at[1], 5, -1, t)
+    sums.append(coefficients(planes - 1))
+    send(beta.at[planes], beta.at[0], 2, 1, t)
+    part_high = smooth(0, planes + 1, above=False)
+    local_part[3] = part_high
+    send(local_part.at[3], local_part.at[0], 4, 1, t)
+    for k in range(1, planes - 1):
+        sums.append(coefficients(k))
+    mass_sum = functools.reduce(lambda a, b: a + b, [m for m, _ in sums])
+    conduct_sum = functools.reduce(lambda a, b: a + b, [c for _, c in sums])
 
     mass_c = coarsen(mass_sum, 0)
     conduct_c = coarsen(conduct_sum, 1)
@@ -167,26 +196,14 @@
     for d in offsets:
         if d != 0:
             send(gam.at[REACH], gam.at[REACH - d], 20 + REACH - d, d, t)
-    for load in loads[2:]:
-        load.wait()
-
-    def smooth(step, k):
-        source = force[step % 2, k]
-        here = prior[step, k + 1]
-        around = beside(here) + (prior[step, k] + prior[step, k + 2])
-        state[step, k + 1] = here + beta[k] * (FORCE_WEIGHT * source - stiff[k] * (6.0 * here - around))
 
     def residual(step):
         total = jnp.zeros((ny, nz), F32)
         for k in range(planes):
-            full, mine = diag[k], state[step, k + 1]
-            mass = full - 6.0 * stiff[k]
-            around = beside(mine)
-            if k > 0:
-                around = around + state[step, k]
-            if k < planes - 1:
-                around = around + state[step, k + 2]
-            total = total + (mass * prior[step, k + 1] + FORCE_WEIGHT * force[step % 2, k]) - (full * mine - stiff[k] * around)
+            full, mine = diag[k], state[step, k + 2]
+            mass = 1.0 + MASS_FLAG * moving[k].astype(F32)
+            around = beside(mine) + (state[step, k + 1] + state[step, k + 3])
+            total = total + (mass * prior[step, k + 2] + FORCE_WEIGHT * force[step % 2, k]) - (full * mine - stiff[k] * around)
         return total
 
     def solve(step, width):
@@ -210,45 +227,51 @@
         product = jnp.dot(stacked, wide[...], preferred_element_type=F32)
         return [product[j * ny:(j + 1) * ny] for j in range(len(errors))]
 
-    def exchange(step):
-        send(state.at[step, 1], state.at[step, top], 3 + 2 * step, -1, t)
-
     for step in range(3):
-        low, high = 2 + 2 * step, 3 + 2 * step
         if step == 0:
-            for k in range(1, planes - 1):
-                smooth(step, k)
-            receive(prior.at[0, 0], 0, -1)
-            smooth(step, 0)
-            send(state.at[step, 1], state.at[step, top], high, -1, t)
+            for i in range(3, planes + 1):
+                state[0, i] = smooth(0, i)
+            receive(prior.at[0, 1], 0, -1)
+            state[0, 2] = local_part[2] + beta[1] * prior[0, 1]
             receive(prior.at[0, top], 1, 1)
-            smooth(step, planes - 1)
-            send(state.at[step, planes], state.at[step, 0], low, 1, t)
-        else:
-            smooth(step, 0)
-            send(state.at[step, 1], state.at[step, top], high, -1, t)
-            smooth(step, planes - 1)
-            send(state.at[step, planes], state.at[step, 0], low, 1, t)
-            for k in range(1, planes - 1):
-                smooth(step, k)
+            state[0, planes + 1] = local_part[3] + beta[planes] * prior[0, top]
+        else:
+            for i in range(3, planes + 1):
+                state[step, i] = smooth(step, i)
+        if step == 0:
+            send(state.at[0, 3], state.at[0, top + 1], 7, -1, t)
+            send(state.at[0, planes], state.at[0, 0], 6, 1, t)
+        elif step == 1:
+            send(state.at[1, 3], came.at[top + 1], 9, -1, ahead)
+            send(state.at[1, planes], came.at[0], 8, 1, ahead)
+        if step == 0:
+            receive(beta.at[0], 2, -1)
+            receive(local_part.at[0], 4, -1)
+            state[0, 1] = local_part[0] + beta[0] * prior[0, 2]
+            receive(beta.at[planes + 1], 3, 1)
+            receive(local_part.at[1], 5, 1)
+            state[0, top] = local_part[1] + beta[planes + 1] * prior[0, planes + 1]
+        else:
+            receive(alpha.at[step % 2, 0], 13 + 2 * step, -1)
+            receive(alpha.at[step % 2, planes + 1], 14 + 2 * step, 1)
+            for i in (1, 2, planes + 1, top):
+                state[step, i] = smooth(step, i)
         if step == 1:
-            send(state.at[step, pl.ds(1, planes)], came.at[pl.ds(1, planes)], 8, 0, ahead)
-        total = residual(step)
-        receive(state.at[step, 0], low, -1)
-        receive(state.at[step, top], high, 1)
-        total = total + stiff[0] * state[step, 0] + stiff[planes - 1] * state[step, top]
-        right = relax_c * coarsen(total, step % 2)
+            send(state.at[1, pl.ds(1, planes + 2)], came.at[pl.ds(1, planes + 2)], 14, 0, ahead)
+        right = relax_c * coarsen(residual(step), step % 2)
         if step == 1:
             own[...] = right
             for d in offsets:
                 send(own, ring.at[step, REACH - d], 40 + REACH - d, d, ahead)
-            send(state.at[step, 0], came.at[0], 9, 0, ahead)
-            send(state.at[step, top], came.at[top], 10, 0, ahead)
         else:
             ring[step, REACH] = right
             for d in offsets:
                 if d != 0 and (step == 0 or abs(d) < REACH):
                     send(ring.at[step, REACH], ring.at[step, REACH - d], 30 + 10 * step + REACH - d, d, t)
+        if step < 2:
+            which = 1 - step
+            send(alpha.at[which, 1], alpha.at[which, planes + 1], 16 + 2 * step, -1, t)
+            send(alpha.at[which, planes], alpha.at[which, 0], 15 + 2 * step, 1, t)
         if step == 0:
             for d in offsets:
                 if d != 0:
@@ -258,21 +281,24 @@
                 receive(ring.at[step, REACH + d], 30 + 10 * step + REACH + d, d)
         if step < 2:
             corrections = expanded(solve(step, 1))
+            if step == 0:
+                receive(state.at[0, 0], 6, -1)
+                receive(state.at[0, top + 1], 7, 1)
+            else:
+                receive(came.at[0], 8, -1)
+                receive(came.at[top + 1], 9, 1)
+                receive(came.at[pl.ds(1, planes + 2)], 14, 0)
+            for i in range(planes + 4):
+                which = 0 if i < 2 else 2 if i >= top else 1
+                base = state[0, i] if step == 0 else came[i]
+                prior[step + 1, i] = base + corrections[which]
             if step == 1:
-                receive(came.at[pl.ds(1, planes)], 8, 0)
-                receive(came.at[0], 9, 0)
-                receive(came.at[top], 10, 0)
-            for k in range(planes + 2):
-                which = 0 if k == 0 else 2 if k == top else 1
-                base = state[0, k] if step == 0 else came[k]
-                prior[step + 1, k] = base + corrections[which]
-            if step == 1:
-                done = pltpu.make_async_copy(prior.at[2, pl.ds(1, planes)], out_starts.at[0], load_sem.at[4])
+                done = pltpu.make_async_copy(prior.at[2, pl.ds(2, planes)], out_starts.at[0], load_sem.at[4])
                 done.start()
         else:
             correction = expanded(solve(step, 0))[0]
             for k in range(planes):
-                final[k] = state[2, k + 1] + correction
+                final[k] = state[2, k + 2] + correction
     last = pltpu.make_async_copy(final, out_interior.at[0], load_sem.at[5])
     last.start()
     for copy, offset in sends:
@@ -298,15 +324,17 @@
             in_specs=[pl.BlockSpec(memory_space=pl.ANY)] * 4,
             out_specs=(pl.BlockSpec(memory_space=pl.ANY),) * 2,
             scratch_shapes=[
-                pltpu.VMEM((3, planes + 2, ny, nz), F32),
-                pltpu.VMEM((3, planes + 2, ny, nz), F32),
-                pltpu.VMEM((planes + 2, ny, nz), F32),
+                pltpu.VMEM((3, planes + 4, ny, nz), F32),
+                pltpu.VMEM((3, planes + 4, ny, nz), F32),
+                pltpu.VMEM((planes + 4, ny, nz), F32),
                 pltpu.VMEM((2,) + block, F32),
                 pltpu.VMEM(block, F32),
                 pltpu.VMEM(block, jnp.int32),
                 pltpu.VMEM(block, F32),
                 pltpu.VMEM(block, F32),
-                pltpu.VMEM(block, F32),
+                pltpu.VMEM((2, planes + 2, ny, nz), F32),
+                pltpu.VMEM((planes + 2, ny, nz), F32),
+                pltpu.VMEM((4, ny, nz), F32),
                 pltpu.VMEM((3, SLOTS) + coarse, F32),
                 pltpu.VMEM(coarse, F32),
                 pltpu.VMEM((SLOTS,) + coarse, F32),
@@ -323,7 +351,7 @@
                 collective_id=0, has_side_effects=True, vmem_limit_bytes=32 * 1024 * 1024
             ),
             name="cycle",
-        )(slab_starts, forcing, density, moving_flags)
+        )(*[pltpu.with_memory_space_constraint(x, pltpu.HBM) for x in (slab_starts, forcing, density, moving_flags)])
 
     placed = (
         P("tm", "space", None, None),

time: 38.5 us -> 32.9 us (0.85)
  the two profiles are of different devices: /device:TPU:1 before, /device:TPU:0 now
where the time goes in v2:
time: 32.9 us; the launch traced here: 32.7 us
  Pallas kernels  30.7 us (93%)
  local copies, waits for them, and re-layouts  1.36 us (4%)
  between operations  0.64 us (2%)
    pallas_call x1, Pallas kernels, local(): pl.pallas_call(functools.partial(kernel, n, nt, planes), out_shape=(resul...  30.7 us
    unnamed x2, local copies, waits for them, and re-layouts  1.36 us

profile of v2, /device:TPU:0, one launch (start us, length us, event | category | flops | bytes accessed | tf_op | source)
XLA Modules:
  0.0 32.7 jit_solution(8203751137067857253)
XLA Ops:
  0.6 30.7 %cycle.1 = (f32[1,4,24,512]{3,2,1,0:T(8,128)S(1)}, f32[1,4,24,512]{3,2,1,0:T(8,128)S(1)}) custom-call(f32[1,4,24,512]{3,2,1,0:T(8,128)} %starts.1, f32[1,2,4,24,512]{4,3,2,1,0:T(8,128)} %forcing.1, f32[4,24,512]{2,1,0:T(8,128)} %density.1, s32[4,24,512]{2,1,0:T(8,128)} %flags.1), custom_call_target="tpu_custom_call" | custom-call | tf_op jit(solution)/shard_map/cycle/pallas_call | solution.py:321
  31.4 0.7 %copy.8 = f32[1,4,24,512]{3,2,1,0:T(8,128)} copy(f32[1,4,24,512]{3,2,1,0:T(8,128)S(1)} %get-tuple-element.4) | data formatting | bytes 393216
  32.1 0.7 %copy.9 = f32[1,4,24,512]{3,2,1,0:T(8,128)} copy(f32[1,4,24,512]{3,2,1,0:T(8,128)S(1)} %get-tuple-element.5) | data formatting | bytes 393216

commit v3 on v2

--- a/solution.py
+++ b/solution.py
@@ -33,7 +33,7 @@
     n, nt, planes,
     starts, forcing, density, flags, out_starts, out_interior,
     prior, state, came, force, rho, moving, stiff, diag, alpha, beta, local_part,
-    ring, own, gam, rows, wide, narrow, spread, final,
+    ring, own, pair, rows, wide, narrow, spread,
     load_sem, send_sem, recv_sem,
 ):
     t = lax.axis_index("tm")
@@ -48,6 +48,7 @@
             return me >= -offset
         return me < n - offset
 
+    order = [1, -1, 3, -3, 2, -2, 4, -4]
     offsets = [d for d in range(-REACH, REACH + 1)]
 
     barrier = pltpu.get_barrier_semaphore()
@@ -96,9 +97,10 @@
 
         @pl.when(jnp.logical_not(inside(d)))
         def _(d=d):
-            zero = jnp.zeros(ring.shape[2:], F32)
-            gam[REACH + d] = zero
-            for step in range(3):
+            zero = jnp.zeros(own.shape, F32)
+            pair[REACH + d, 0] = zero
+            pair[REACH + d, 1] = zero
+            for step in range(2):
                 ring[step, REACH + d] = zero
             if abs(d) == 1:
                 side = 0 if d < 0 else 1
@@ -185,6 +187,12 @@
     send(local_part.at[3], local_part.at[0], 4, 1, t)
     for k in range(1, planes - 1):
         sums.append(coefficients(k))
+    for i in range(3, planes + 1):
+        state[0, i] = smooth(0, i)
+    send(state.at[0, 3], state.at[0, top + 1], 7, -1, t)
+    send(state.at[0, planes], state.at[0, 0], 6, 1, t)
+    send(alpha.at[1, 1], alpha.at[1, planes + 1], 16, -1, t)
+    send(alpha.at[1, planes], alpha.at[1, 0], 15, 1, t)
     mass_sum = functools.reduce(lambda a, b: a + b, [m for m, _ in sums])
     conduct_sum = functools.reduce(lambda a, b: a + b, [c for _, c in sums])
 
@@ -192,10 +200,7 @@
     conduct_c = coarsen(conduct_sum, 1)
     real = lax.broadcasted_iota(jnp.int32, (ncy, ncz), 0) < ny // 4
     relax_c = jnp.where(real, RELAX / jnp.where(real, mass_c + 6.0 * COARSE_STIFF * conduct_c, 1.0), 0.0)
-    gam[REACH] = COARSE_STIFF * conduct_c * relax_c
-    for d in offsets:
-        if d != 0:
-            send(gam.at[REACH], gam.at[REACH - d], 20 + REACH - d, d, t)
+    pair[REACH, 1] = COARSE_STIFF * conduct_c * relax_c
 
     def residual(step):
         total = jnp.zeros((ny, nz), F32)
@@ -207,7 +212,10 @@
         return total
 
     def solve(step, width):
-        right = {i: ring[step, i] for i in range(1 - width, SLOTS - 1 + width)}
+        gam = {i: pair[i, 1] for i in range(1, SLOTS - 1)}
+        right = {
+            i: pair[i, 0] if step == 0 else ring[step - 1, i] for i in range(1 - width, SLOTS - 1 + width)
+        }
         error = right
         for sweep in range(COARSE_SWEEPS - 1):
             reach = COARSE_SWEEPS - 2 - sweep + width
@@ -229,8 +237,6 @@
 
     for step in range(3):
         if step == 0:
-            for i in range(3, planes + 1):
-                state[0, i] = smooth(0, i)
             receive(prior.at[0, 1], 0, -1)
             state[0, 2] = local_part[2] + beta[1] * prior[0, 1]
             receive(prior.at[0, top], 1, 1)
@@ -238,10 +244,7 @@
         else:
             for i in range(3, planes + 1):
                 state[step, i] = smooth(step, i)
-        if step == 0:
-            send(state.at[0, 3], state.at[0, top + 1], 7, -1, t)
-            send(state.at[0, planes], state.at[0, 0], 6, 1, t)
-        elif step == 1:
+        if step == 1:
             send(state.at[1, 3], came.at[top + 1], 9, -1, ahead)
             send(state.at[1, planes], came.at[0], 8, 1, ahead)
         if step == 0:
@@ -259,26 +262,26 @@
         if step == 1:
             send(state.at[1, pl.ds(1, planes + 2)], came.at[pl.ds(1, planes + 2)], 14, 0, ahead)
         right = relax_c * coarsen(residual(step), step % 2)
-        if step == 1:
+        if step == 0:
+            pair[REACH, 0] = right
+            for d in order:
+                send(pair.at[REACH], pair.at[REACH - d], 20 + REACH - d, d, t)
+            for d in order:
+                receive(pair.at[REACH + d], 20 + REACH + d, d)
+            send(alpha.at[0, 1], alpha.at[0, planes + 1], 18, -1, t)
+            send(alpha.at[0, planes], alpha.at[0, 0], 17, 1, t)
+        elif step == 1:
             own[...] = right
-            for d in offsets:
-                send(own, ring.at[step, REACH - d], 40 + REACH - d, d, ahead)
-        else:
-            ring[step, REACH] = right
-            for d in offsets:
-                if d != 0 and (step == 0 or abs(d) < REACH):
-                    send(ring.at[step, REACH], ring.at[step, REACH - d], 30 + 10 * step + REACH - d, d, t)
-        if step < 2:
-            which = 1 - step
-            send(alpha.at[which, 1], alpha.at[which, planes + 1], 16 + 2 * step, -1, t)
-            send(alpha.at[which, planes], alpha.at[which, 0], 15 + 2 * step, 1, t)
-        if step == 0:
-            for d in offsets:
-                if d != 0:
-                    receive(gam.at[REACH + d], 20 + REACH + d, d)
-        for d in offsets:
-            if (d != 0 or step == 1) and (step < 2 or abs(d) < REACH):
-                receive(ring.at[step, REACH + d], 30 + 10 * step + REACH + d, d)
+            for d in order + [0]:
+                send(own, ring.at[0, REACH - d], 30 + REACH - d, d, ahead)
+            for d in order + [0]:
+                receive(ring.at[0, REACH + d], 30 + REACH + d, d)
+        else:
+            ring[1, REACH] = right
+            for d in order[:-2]:
+                send(ring.at[1, REACH], ring.at[1, REACH - d], 40 + REACH - d, d, t)
+            for d in order[:-2]:
+                receive(ring.at[1, REACH + d], 40 + REACH + d, d)
         if step < 2:
             corrections = expanded(solve(step, 1))
             if step == 0:
@@ -293,21 +296,17 @@
                 base = state[0, i] if step == 0 else came[i]
                 prior[step + 1, i] = base + corrections[which]
             if step == 1:
-                done = pltpu.make_async_copy(prior.at[2, pl.ds(2, planes)], out_starts.at[0], load_sem.at[4])
-                done.start()
+                for k in range(planes):
+                    out_starts[0, k] = prior[2, k + 2]
         else:
             correction = expanded(solve(step, 0))[0]
             for k in range(planes):
-                final[k] = state[2, k + 2] + correction
-    last = pltpu.make_async_copy(final, out_interior.at[0], load_sem.at[5])
-    last.start()
+                out_interior[0, k] = state[2, k + 2] + correction
     for copy, offset in sends:
         if offset == 0:
             copy.wait_send()
         else:
             pl.when(inside(offset))(lambda copy=copy: copy.wait_send())
-    done.wait()
-    last.wait()
 
 
 def solution(mesh):
@@ -322,7 +321,7 @@
             functools.partial(kernel, n, nt, planes),
             out_shape=(result, result),
             in_specs=[pl.BlockSpec(memory_space=pl.ANY)] * 4,
-            out_specs=(pl.BlockSpec(memory_space=pl.ANY),) * 2,
+            out_specs=(pl.BlockSpec(memory_space=pltpu.VMEM),) * 2,
             scratch_shapes=[
                 pltpu.VMEM((3, planes + 4, ny, nz), F32),
                 pltpu.VMEM((3, planes + 4, ny, nz), F32),
@@ -335,14 +334,13 @@
                 pltpu.VMEM((2, planes + 2, ny, nz), F32),
                 pltpu.VMEM((planes + 2, ny, nz), F32),
                 pltpu.VMEM((4, ny, nz), F32),
-                pltpu.VMEM((3, SLOTS) + coarse, F32),
+                pltpu.VMEM((2, SLOTS) + coarse, F32),
                 pltpu.VMEM(coarse, F32),
-                pltpu.VMEM((SLOTS,) + coarse, F32),
+                pltpu.VMEM((SLOTS, 2) + coarse, F32),
                 pltpu.VMEM((2, 32, nz // 4), F32),
                 pltpu.VMEM((3 * nz // 4, nz), BF16),
                 pltpu.VMEM((nz, nz // 4), BF16),
                 pltpu.VMEM((3, 32, nz // 4), F32),
-                pltpu.VMEM(block, F32),
                 pltpu.SemaphoreType.DMA((6,)),
                 pltpu.SemaphoreType.DMA((60,)),
                 pltpu.SemaphoreType.DMA((60,)),

time: 32.9 us -> 31.2 us (0.948)
  Pallas kernels: 30.7 us -> 28.8 us
    pallas_call x1, Pallas kernels: 30.7 us -> 28.8 us  [local(): pl.pallas_call(functools.partial(kernel, n, nt, planes), out_shape=(resul...]
where the time goes in v3:
time: 31.2 us; the launch traced here: 30.8 us
  Pallas kernels  28.8 us (92%)
  local copies, waits for them, and re-layouts  1.36 us (4%)
  between operations  0.64 us (2%)
    pallas_call x1, Pallas kernels, local(): pl.pallas_call(functools.partial(kernel, n, nt, planes), out_shape=(resul...  28.8 us
    unnamed x2, local copies, waits for them, and re-layouts  1.36 us

profile of v3, /device:TPU:0, one launch (start us, length us, event | category | flops | bytes accessed | tf_op | source)
XLA Modules:
  0.0 30.8 jit_solution(5604227426851301513)
XLA Ops:
  0.6 28.8 %cycle.1 = (f32[1,4,24,512]{3,2,1,0:T(8,128)S(1)}, f32[1,4,24,512]{3,2,1,0:T(8,128)S(1)}) custom-call(f32[1,4,24,512]{3,2,1,0:T(8,128)} %starts.1, f32[1,2,4,24,512]{4,3,2,1,0:T(8,128)} %forcing.1, f32[4,24,512]{2,1,0:T(8,128)} %density.1, s32[4,24,512]{2,1,0:T(8,128)} %flags.1), custom_call_target="tpu_custom_call" | custom-call | tf_op jit(solution)/shard_map/cycle/pallas_call | solution.py:320
  29.5 0.7 %copy.8 = f32[1,4,24,512]{3,2,1,0:T(8,128)} copy(f32[1,4,24,512]{3,2,1,0:T(8,128)S(1)} %get-tuple-element.4) | data formatting | bytes 393216
  30.1 0.7 %copy.9 = f32[1,4,24,512]{3,2,1,0:T(8,128)} copy(f32[1,4,24,512]{3,2,1,0:T(8,128)S(1)} %get-tuple-element.5) | data formatting | bytes 393216

commit v4 on v3

--- a/solution.py
+++ b/solution.py
@@ -110,7 +110,6 @@
                 beta[side * (planes + 1)] = fine_zero
                 alpha[0, side * (planes + 1)] = fine_zero
                 alpha[1, side * (planes + 1)] = fine_zero
-                state[0, side * (top + 1)] = fine_zero
                 came[side * (top + 1)] = fine_zero
 
     narrow[...] = (
@@ -189,10 +188,8 @@
         sums.append(coefficients(k))
     for i in range(3, planes + 1):
         state[0, i] = smooth(0, i)
-    send(state.at[0, 3], state.at[0, top + 1], 7, -1, t)
-    send(state.at[0, planes], state.at[0, 0], 6, 1, t)
-    send(alpha.at[1, 1], alpha.at[1, planes + 1], 16, -1, t)
-    send(alpha.at[1, planes], alpha.at[1, 0], 15, 1, t)
+    local_part[4] = alpha[1, 1] + beta[1] * state[0, 3]
+    local_part[5] = alpha[1, planes] + beta[planes] * state[0, planes]
     mass_sum = functools.reduce(lambda a, b: a + b, [m for m, _ in sums])
     conduct_sum = functools.reduce(lambda a, b: a + b, [c for _, c in sums])
 
@@ -266,6 +263,8 @@
             pair[REACH, 0] = right
             for d in order:
                 send(pair.at[REACH], pair.at[REACH - d], 20 + REACH - d, d, t)
+            send(local_part.at[4], alpha.at[1, planes + 1], 16, -1, t)
+            send(local_part.at[5], alpha.at[1, 0], 15, 1, t)
             for d in order:
                 receive(pair.at[REACH + d], 20 + REACH + d, d)
             send(alpha.at[0, 1], alpha.at[0, planes + 1], 18, -1, t)
@@ -284,15 +283,15 @@
                 receive(ring.at[1, REACH + d], 40 + REACH + d, d)
         if step < 2:
             corrections = expanded(solve(step, 1))
-            if step == 0:
-                receive(state.at[0, 0], 6, -1)
-                receive(state.at[0, top + 1], 7, 1)
-            else:
+            if step == 1:
                 receive(came.at[0], 8, -1)
                 receive(came.at[top + 1], 9, 1)
                 receive(came.at[pl.ds(1, planes + 2)], 14, 0)
             for i in range(planes + 4):
                 which = 0 if i < 2 else 2 if i >= top else 1
+                if step == 0 and i in (0, top + 1):
+                    prior[1, i] = corrections[which]
+                    continue
                 base = state[0, i] if step == 0 else came[i]
                 prior[step + 1, i] = base + corrections[which]
             if step == 1:
@@ -333,7 +332,7 @@
                 pltpu.VMEM(block, F32),
                 pltpu.VMEM((2, planes + 2, ny, nz), F32),
                 pltpu.VMEM((planes + 2, ny, nz), F32),
-                pltpu.VMEM((4, ny, nz), F32),
+                pltpu.VMEM((6, ny, nz), F32),
                 pltpu.VMEM((2, SLOTS) + coarse, F32),
                 pltpu.VMEM(coarse, F32),
                 pltpu.VMEM((SLOTS, 2) + coarse, F32),

time: 31.2 us -> 29.5 us (0.946)
  Pallas kernels: 28.8 us -> 27 us
    pallas_call x1, Pallas kernels: 28.8 us -> 27 us  [local(): pl.pallas_call(functools.partial(kernel, n, nt, planes), out_shape=(resul...]
where the time goes in v4:
time: 29.5 us; the launch traced here: 29 us
  Pallas kernels  27 us (92%)
  local copies, waits for them, and re-layouts  1.36 us (5%)
  between operations  0.64 us (2%)
    pallas_call x1, Pallas kernels, local(): pl.pallas_call(functools.partial(kernel, n, nt, planes), out_shape=(resul...  27 us
    unnamed x2, local copies, waits for them, and re-layouts  1.36 us

profile of v4, /device:TPU:0, one launch (start us, length us, event | category | flops | bytes accessed | tf_op | source)
XLA Modules:
  0.0 29.0 jit_solution(16956114902661520164)
XLA Ops:
  0.6 27.0 %cycle.1 = (f32[1,4,24,512]{3,2,1,0:T(8,128)S(1)}, f32[1,4,24,512]{3,2,1,0:T(8,128)S(1)}) custom-call(f32[1,4,24,512]{3,2,1,0:T(8,128)} %starts.1, f32[1,2,4,24,512]{4,3,2,1,0:T(8,128)} %forcing.1, f32[4,24,512]{2,1,0:T(8,128)} %density.1, s32[4,24,512]{2,1,0:T(8,128)} %flags.1), custom_call_target="tpu_custom_call" | custom-call | tf_op jit(solution)/shard_map/cycle/pallas_call | solution.py:319
  27.6 0.7 %copy.8 = f32[1,4,24,512]{3,2,1,0:T(8,128)} copy(f32[1,4,24,512]{3,2,1,0:T(8,128)S(1)} %get-tuple-element.4) | data formatting | bytes 393216
  28.3 0.7 %copy.9 = f32[1,4,24,512]{3,2,1,0:T(8,128)} copy(f32[1,4,24,512]{3,2,1,0:T(8,128)S(1)} %get-tuple-element.5) | data formatting | bytes 393216

commit v5 on v4

--- a/solution.py
+++ b/solution.py
@@ -39,9 +39,13 @@
     t = lax.axis_index("tm")
     me = lax.axis_index("space")
     ahead, behind = lax.rem(t + 1, nt), lax.rem(t + nt - 1, nt)
+    half = lax.rem(t, 2)
+    mate = t + 1 - 2 * half
     top = planes + 2
     ny, nz = prior.shape[-2:]
     ncy, ncz = 8, nz // 4
+    mine = pl.ds(pl.multiple_of(half * (nz // 2), nz // 2), nz // 2)
+    theirs = pl.ds(pl.multiple_of((1 - half) * (nz // 2), nz // 2), nz // 2)
 
     def inside(offset):
         if offset < 0:
@@ -58,6 +62,7 @@
             pl.semaphore_signal(barrier, inc=1, device_id=(t, me + d), device_id_type=MESH)
             pl.semaphore_signal(barrier, inc=1, device_id=(behind, me + d), device_id_type=MESH)
     pl.semaphore_signal(barrier, inc=1, device_id=(behind, me), device_id_type=MESH)
+    pl.semaphore_signal(barrier, inc=1, device_id=(ahead, me), device_id_type=MESH)
 
     loads = [
         pltpu.make_async_copy(density, rho, load_sem.at[0]),
@@ -82,6 +87,11 @@
             copy.start()
         else:
             pl.when(inside(offset))(lambda: copy.start())
+        sends.append((copy, offset))
+
+    def pass_on(part, k, offset):
+        copy = copy_to(part, part, k, (mate, me))
+        pl.when(inside(offset))(lambda: copy.start())
         sends.append((copy, offset))
 
     def receive(dst, k, offset):
@@ -146,9 +156,7 @@
         parts = [rows[slot, pl.ds(k, ncy, stride=4), :] for k in range(4)]
         return ((parts[0] + parts[1]) + (parts[2] + parts[3])) * (1.0 / 64.0)
 
-    pl.semaphore_wait(barrier, 1 + 2 * sum(inside(d).astype(jnp.int32) for d in offsets if d != 0))
-    send(starts.at[0, 0], prior.at[0, top], 1, -1, t)
-    send(starts.at[0, planes - 1], prior.at[0, 1], 0, 1, t)
+    pl.semaphore_wait(barrier, 2 + 2 * sum(inside(d).astype(jnp.int32) for d in offsets if d != 0))
 
     for load in loads:
         load.wait()
@@ -175,12 +183,14 @@
         return here + (alpha[step % 2, i - 1] + beta[i - 1] * (around - 6.0 * here))
 
     sums = [coefficients(0)]
-    send(beta.at[1], beta.at[planes + 1], 3, -1, t)
+    send(beta.at[1, :, mine], beta.at[planes + 1, :, mine], 3, -1, t)
+    sums.append(coefficients(planes - 1))
+    send(beta.at[planes, :, mine], beta.at[0, :, mine], 2, 1, t)
+    send(starts.at[0, 0], prior.at[0, top], 1, -1, t)
+    send(starts.at[0, planes - 1], prior.at[0, 1], 0, 1, t)
     part_low = smooth(0, 2, below=False)
     local_part[2] = part_low
     send(local_part.at[2], local_part.at[1], 5, -1, t)
-    sums.append(coefficients(planes - 1))
-    send(beta.at[planes], beta.at[0], 2, 1, t)
     part_high = smooth(0, planes + 1, above=False)
     local_part[3] = part_high
     send(local_part.at[3], local_part.at[0], 4, 1, t)
@@ -234,6 +244,10 @@
 
     for step in range(3):
         if step == 0:
+            receive(beta.at[0, :, mine], 2, -1)
+            pass_on(beta.at[0, :, mine], 6, -1)
+            receive(beta.at[planes + 1, :, mine], 3, 1)
+            pass_on(beta.at[planes + 1, :, mine], 7, 1)
             receive(prior.at[0, 1], 0, -1)
             state[0, 2] = local_part[2] + beta[1] * prior[0, 1]
             receive(prior.at[0, top], 1, 1)
@@ -245,10 +259,10 @@
             send(state.at[1, 3], came.at[top + 1], 9, -1, ahead)
             send(state.at[1, planes], came.at[0], 8, 1, ahead)
         if step == 0:
-            receive(beta.at[0], 2, -1)
+            receive(beta.at[0, :, theirs], 6, -1)
             receive(local_part.at[0], 4, -1)
             state[0, 1] = local_part[0] + beta[0] * prior[0, 2]
-            receive(beta.at[planes + 1], 3, 1)
+            receive(beta.at[planes + 1, :, theirs], 7, 1)
             receive(local_part.at[1], 5, 1)
             state[0, top] = local_part[1] + beta[planes + 1] * prior[0, planes + 1]
         else:

time: 29.5 us -> 28 us (0.949); the launches traced: 29 us -> 27.8 us
  Pallas kernels: 27 us -> 25.8 us
    pallas_call x1, Pallas kernels: 27 us -> 25.8 us  [local(): pl.pallas_call(functools.partial(kernel, n, nt, planes), out_shape=(resul...]
where the time goes in v5:
time: 28 us; the launch traced here: 27.8 us
  Pallas kernels  25.8 us (92%)
  local copies, waits for them, and re-layouts  1.36 us (5%)
  between operations  0.64 us (2%)
    pallas_call x1, Pallas kernels, local(): pl.pallas_call(functools.partial(kernel, n, nt, planes), out_shape=(resul...  25.8 us
    unnamed x2, local copies, waits for them, and re-layouts  1.36 us

profile of v5, /device:TPU:0, one launch (start us, length us, event | category | flops | bytes accessed | tf_op | source)
XLA Modules:
  0.0 27.8 jit_solution(18076668820531771707)
XLA Ops:
  0.6 25.8 %cycle.1 = (f32[1,4,24,512]{3,2,1,0:T(8,128)S(1)}, f32[1,4,24,512]{3,2,1,0:T(8,128)S(1)}) custom-call(f32[1,4,24,512]{3,2,1,0:T(8,128)} %starts.1, f32[1,2,4,24,512]{4,3,2,1,0:T(8,128)} %forcing.1, f32[4,24,512]{2,1,0:T(8,128)} %density.1, s32[4,24,512]{2,1,0:T(8,128)} %flags.1), custom_call_target="tpu_custom_call" | custom-call | tf_op jit(solution)/shard_map/cycle/pallas_call | solution.py:333
  26.5 0.7 %copy.8 = f32[1,4,24,512]{3,2,1,0:T(8,128)} copy(f32[1,4,24,512]{3,2,1,0:T(8,128)S(1)} %get-tuple-element.4) | data formatting | bytes 393216
  27.1 0.7 %copy.9 = f32[1,4,24,512]{3,2,1,0:T(8,128)} copy(f32[1,4,24,512]{3,2,1,0:T(8,128)S(1)} %get-tuple-element.5) | data formatting | bytes 393216

commit v6 on v5

--- a/solution.py
+++ b/solution.py
@@ -281,12 +281,12 @@
             send(local_part.at[5], alpha.at[1, 0], 15, 1, t)
             for d in order:
                 receive(pair.at[REACH + d], 20 + REACH + d, d)
-            send(alpha.at[0, 1], alpha.at[0, planes + 1], 18, -1, t)
-            send(alpha.at[0, planes], alpha.at[0, 0], 17, 1, t)
         elif step == 1:
             own[...] = right
             for d in order + [0]:
                 send(own, ring.at[0, REACH - d], 30 + REACH - d, d, ahead)
+            send(alpha.at[0, 1], alpha.at[0, planes + 1], 18, -1, t)
+            send(alpha.at[0, planes], alpha.at[0, 0], 17, 1, t)
             for d in order + [0]:
                 receive(ring.at[0, REACH + d], 30 + REACH + d, d)
         else:

time: 28 us -> 29.2 us (1.043)
  Pallas kernels: 25.8 us -> 27 us
    pallas_call x1, Pallas kernels: 25.8 us -> 27 us  [local(): pl.pallas_call(functools.partial(kernel, n, nt, planes), out_shape=(resul...]
where the time goes in v6:
time: 29.2 us; the launch traced here: 29 us
  Pallas kernels  27 us (92%)
  local copies, waits for them, and re-layouts  1.36 us (5%)
  between operations  0.64 us (2%)
    pallas_call x1, Pallas kernels, local(): pl.pallas_call(functools.partial(kernel, n, nt, planes), out_shape=(resul...  27 us
    unnamed x2, local copies, waits for them, and re-layouts  1.36 us

profile of v6, /device:TPU:0, one launch (start us, length us, event | category | flops | bytes accessed | tf_op | source)
XLA Modules:
  0.0 29.0 jit_solution(9990779922067075099)
XLA Ops:
  0.6 27.0 %cycle.1 = (f32[1,4,24,512]{3,2,1,0:T(8,128)S(1)}, f32[1,4,24,512]{3,2,1,0:T(8,128)S(1)}) custom-call(f32[1,4,24,512]{3,2,1,0:T(8,128)} %starts.1, f32[1,2,4,24,512]{4,3,2,1,0:T(8,128)} %forcing.1, f32[4,24,512]{2,1,0:T(8,128)} %density.1, s32[4,24,512]{2,1,0:T(8,128)} %flags.1), custom_call_target="tpu_custom_call" | custom-call | tf_op jit(solution)/shard_map/cycle/pallas_call | solution.py:333
  27.7 0.7 %copy.8 = f32[1,4,24,512]{3,2,1,0:T(8,128)} copy(f32[1,4,24,512]{3,2,1,0:T(8,128)S(1)} %get-tuple-element.4) | data formatting | bytes 393216
  28.3 0.7 %copy.9 = f32[1,4,24,512]{3,2,1,0:T(8,128)} copy(f32[1,4,24,512]{3,2,1,0:T(8,128)S(1)} %get-tuple-element.5) | data formatting | bytes 393216
